TPU v7x, 256 devices: a whole 4x4x8 slice. The times are simulated.
256 devices in a mesh: lon: 32 (over z_hi, y, core), lat: 8 (over x, z_lo).
Axes of the slice: x: 4, y: 4, z: 8 (z_hi: 4, z_lo: 2; z = z_hi * 2 + z_lo), core: 2. Of those that a mesh axis runs over, the one named last changes fastest.
Arguments:
- temp: float32 [16, 1024, 4096], P(None, 'lat', 'lon'), may hold values from -6 to 6
- salt: float32 [16, 1024, 4096], P(None, 'lat', 'lon'), may hold values from -6 to 6
- uvel: float32 [16, 1024, 4096], P(None, 'lat', 'lon'), may hold values from -6 to 6
- vvel: float32 [16, 1024, 4096], P(None, 'lat', 'lon'), may hold values from -6 to 6
- depth_levels: int32 [1024, 4096], P('lat', 'lon'), may hold values from 0 to 16
Outputs:
- temp_next: float32 [16, 1024, 4096], P(None, 'lat', 'lon')
- salt_next: float32 [16, 1024, 4096], P(None, 'lat', 'lon')
- uvel_next: float32 [16, 1024, 4096], P(None, 'lat', 'lon')
- vvel_next: float32 [16, 1024, 4096], P(None, 'lat', 'lon')
Inputs may be any that keep to these rules, and one draw needn't show every extreme that they name: `depth_levels`: wet levels are counted from the top.
All inputs are finite; a program needn't handle non-finite values.
Results may differ from a plain program's by a relative error of at most 0.0003.
Values sent between devices are 32-bit elements; how exact they have to be, the bound alone decides.
A program may use at most 128 MiB of HBM per device.

v0:
```python
import math

import jax
import jax.numpy as jnp
from jax import lax
from jax.sharding import PartitionSpec as P

time_step = 0.2
biharmonic = 0.01


def from_partner(value, axis, bit):
    mask = 2**bit
    pairs = [(source, source ^ mask) for source in range(lax.axis_size(axis))]
    return lax.ppermute(value, axis, pairs)


def padded(cells, sides, width, closed):
    for axis, dim in sides:
        count = lax.axis_size(axis)
        ends = count if closed else count - 1
        head = lax.slice_in_dim(cells, 0, width, axis=dim)
        tail = lax.slice_in_dim(cells, cells.shape[dim] - width, cells.shape[dim], axis=dim)
        cells = jnp.concatenate(
            [
                lax.ppermute(tail, axis, [(i, (i + 1) % count) for i in range(ends)]),
                cells,
                lax.ppermute(head, axis, [((i + 1) % count, i) for i in range(ends)]),
            ],
            axis=dim,
        )
    return cells


def laplace(grid):
    return (
        grid[..., 2:, 1:-1]
        + grid[..., :-2, 1:-1]
        + grid[..., 1:-1, 2:]
        + grid[..., 1:-1, :-2]
        - 4.0 * grid[..., 1:-1, 1:-1]
    )


def advance(extended, pres, wet, coriolis):
    centre = extended[..., 2:-2, 2:-2]
    east = extended[..., 2:-2, 3:-1]
    west = extended[..., 2:-2, 1:-3]
    north = extended[..., 3:-1, 2:-2]
    south = extended[..., 1:-3, 2:-2]
    first = centre[2]
    second = centre[3]
    carried = 0.5 * (first * (east - west) + second * (north - south))
    smooth = laplace(laplace(extended))
    grad_x = 0.5 * (pres[..., 2:-2, 3:-1] - pres[..., 2:-2, 1:-3])
    grad_y = 0.5 * (pres[..., 3:-1, 2:-2] - pres[..., 1:-3, 2:-2])
    temp_new = centre[0] - time_step * carried[0] - biharmonic * smooth[0]
    salt_new = centre[1] - time_step * carried[1] - biharmonic * smooth[1]
    first_new = (
        first + time_step * (coriolis * second - grad_x - carried[2]) - biharmonic * smooth[2]
    )
    second_new = (
        second + time_step * (-coriolis * first - grad_y - carried[3]) - biharmonic * smooth[3]
    )
    return jnp.stack([temp_new, salt_new, first_new, second_new]) * wet


def mirror_rows(piece):
    count_bits = lax.axis_size("lon").bit_length() - 1
    for bit in range(count_bits):
        piece = from_partner(piece, "lon", bit)
    return piece


def shards(temp, salt, uvel, vvel, depth_levels):
    levels = temp.shape[0]
    rows_dev = temp.shape[1]
    level_index = jnp.arange(levels, dtype=jnp.int32)[:, None, None]
    wet = jnp.where(depth_levels[None] > level_index, 1.0, 0.0).astype(jnp.float32)
    data = jnp.stack([temp, salt, uvel, vvel]) * wet
    signs = jnp.array([1.0, 1.0, -1.0, -1.0], jnp.float32)[:, None, None, None]
    at_north = lax.axis_index("lat") == lax.axis_size("lat") - 1
    rows = padded(data, (("lat", 2),), 2, False)
    piece = data[:, :, -2:, :][:, :, ::-1, ::-1] * signs
    folded = mirror_rows(piece)
    rows = rows.at[:, :, -2:, :].set(jnp.where(at_north, folded, rows[:, :, -2:, :]))
    extended = padded(rows, (("lon", 3),), 2, True)
    density = -0.2 * extended[0] + 0.8 * extended[1]
    pres = jnp.cumsum(density, axis=0) - 0.5 * density
    total_rows = rows_dev * lax.axis_size("lat")
    global_rows = (lax.axis_index("lat") * rows_dev + jnp.arange(rows_dev, dtype=jnp.int32)).astype(
        jnp.float32
    )
    coriolis = (0.5 * jnp.sin(math.pi * (global_rows + 0.5) / total_rows - 0.5 * math.pi))[:, None]
    result = advance(extended, pres, wet, coriolis)
    return (result[0], result[1], result[2], result[3])


def solution(mesh):
    placed = (
        P(None, "lat", "lon"),
        P(None, "lat", "lon"),
        P(None, "lat", "lon"),
        P(None, "lat", "lon"),
        P("lat", "lon"),
    )
    return jax.shard_map(
        shards,
        mesh=mesh,
        in_specs=placed,
        out_specs=(
            P(None, "lat", "lon"),
            P(None, "lat", "lon"),
            P(None, "lat", "lon"),
            P(None, "lat", "lon"),
        ),
        check_vma=False,
    )
```

profile of v0, /device:TPU:4, one launch (start us, length us, event | category | flops | bytes accessed | tf_op | source)
XLA Modules:
  0.0 118.5 jit_solution(9448723048142292274)
XLA Ops:
  0.6 0.9 fusion.30
  1.6 0.0 copy-start.6
  1.6 2.6 %maximum_multiply_fusion = f32[4,16,128,128]{3,2,1,0:T(8,128)S(1)} fusion(f32[1,16,128,128]{3,2,1,0:T(8,128)} %bitcast.68, f32[1,16,128,128]{3,2,1,0:T(8,128)} %bitcast.69, f32[1,16,128,128]{3,2,1,0:T(8,128)} %bitcast.70, f32[1,16,128,128]{3,2,1,0:T(8,128)} %bitcast.71, f32[16,128,128]{2,1,0:T(8,128)S(1)} %fusion.30), kind=kLoop, calls=%fused_computation.20 | loop fusion | flops 4194304 | bytes 9437184 | tf_op jit(solution)/shard_map/mul | solution.py:80
  4.2 0.0 copy-start.3
  4.2 1.9 %copy-done.3 = f32[4,16,128,128]{3,2,1,0:T(8,128)} copy-done((f32[4,16,128,128]{3,2,1,0:T(8,128)}, f32[4,16,128,128]{3,2,1,0:T(8,128)S(1)}, u32[]{:S(2)}) %copy-start.3) | copy-done | bytes 4194328
  6.2 0.3 rev.3
  6.5 0.0 copy-done.6
  6.5 0.1 broadcast_multiply_fusion
  6.6 0.1 collective-permute-start.2
  6.7 1.2 %collective-permute-done.2 = f32[4,16,2,128]{3,2,1,0:T(2,128)S(1)} collective-permute-done((f32[4,16,2,128]{3,2,1,0:T(2,128)S(1)}, f32[4,16,2,128]{3,2,1,0:T(2,128)S(1)}, u32[]{:S(2)}, u32[]{:S(2)}) %collective-permute-start.2) | collective-permute-done | bytes 65568 | tf_op jit(solution)/shard_map/ppermute | solution.py:15
  7.9 1.6 %collective-permute-start.3 = (f32[4,16,2,128]{3,2,1,0:T(2,128)S(1)}, f32[4,16,2,128]{3,2,1,0:T(2,128)S(1)}, u32[]{:S(2)}, u32[]{:S(2)}) collective-permute-start(f32[4,16,2,128]{3,2,1,0:T(2,128)S(1)} %collective-permute-done.2), channel_id=1, source_target_pairs={{0,16},{8,24},{16,0},{24,8},{32,48},{40,56},{48,32},{56,40},{64,80... | collective-permute-start | bytes 196616 | tf_op jit(solution)/shard_map/ppermute | solution.py:15
  9.5 2.7 %collective-permute-done.3 = f32[4,16,2,128]{3,2,1,0:T(2,128)S(1)} collective-permute-done((f32[4,16,2,128]{3,2,1,0:T(2,128)S(1)}, f32[4,16,2,128]{3,2,1,0:T(2,128)S(1)}, u32[]{:S(2)}, u32[]{:S(2)}) %collective-permute-start.3) | collective-permute-done | bytes 65568 | tf_op jit(solution)/shard_map/ppermute | solution.py:15
  12.2 3.2 %collective-permute-start.4 = (f32[4,16,2,128]{3,2,1,0:T(2,128)S(1)}, f32[4,16,2,128]{3,2,1,0:T(2,128)S(1)}, u32[]{:S(2)}, u32[]{:S(2)}) collective-permute-start(f32[4,16,2,128]{3,2,1,0:T(2,128)S(1)} %collective-permute-done.3), channel_id=1, source_target_pairs={{0,32},{8,40},{16,48},{24,56},{32,0},{40,8},{48,16},{56,24},{64,96... | collective-permute-start | bytes 196616 | tf_op jit(solution)/shard_map/ppermute | solution.py:15
  15.4 3.8 %collective-permute-start = (f32[4,16,2,128]{3,2,1,0:T(2,128)S(1)}, f32[4,16,2,128]{3,2,1,0:T(2,128)S(1)}, u32[]{:S(2)}, u32[]{:S(2)}) collective-permute-start(f32[4,16,2,128]{3,2,1,0:T(2,128)S(1)} %get-tuple-element.28), channel_id=1, source_target_pairs={{0,1},{1,2},{2,3},{3,4},{4,5},{5,6},{6,7},{8,9},{9,10},{10,11},{11... | collective-permute-start | bytes 196616 | tf_op jit(solution)/shard_map/ppermute | solution.py:26
  19.2 2.9 %collective-permute-start.1 = (f32[4,16,2,128]{3,2,1,0:T(2,128)S(1)}, f32[4,16,2,128]{3,2,1,0:T(2,128)S(1)}, u32[]{:S(2)}, u32[]{:S(2)}) collective-permute-start(f32[4,16,2,128]{3,2,1,0:T(2,128)S(1)} %get-tuple-element.29), channel_id=1, source_target_pairs={{1,0},{2,1},{3,2},{4,3},{5,4},{6,5},{7,6},{9,8},{10,9},{11,10},{12... | collective-permute-start | bytes 196616 | tf_op jit(solution)/shard_map/ppermute | solution.py:28
  22.2 0.0 collective-permute-done.4
  22.2 3.4 %collective-permute-start.5 = (f32[4,16,2,128]{3,2,1,0:T(2,128)S(1)}, f32[4,16,2,128]{3,2,1,0:T(2,128)S(1)}, u32[]{:S(2)}, u32[]{:S(2)}) collective-permute-start(f32[4,16,2,128]{3,2,1,0:T(2,128)S(1)} %collective-permute-done.4), channel_id=1, source_target_pairs={{0,64},{8,72},{16,80},{24,88},{32,96},{40,104},{48,112},{56,120},{... | collective-permute-start | bytes 196616 | tf_op jit(solution)/shard_map/ppermute | solution.py:15
  25.6 2.2 %collective-permute-done.5 = f32[4,16,2,128]{3,2,1,0:T(2,128)S(1)} collective-permute-done((f32[4,16,2,128]{3,2,1,0:T(2,128)S(1)}, f32[4,16,2,128]{3,2,1,0:T(2,128)S(1)}, u32[]{:S(2)}, u32[]{:S(2)}) %collective-permute-start.5) | collective-permute-done | bytes 65568 | tf_op jit(solution)/shard_map/ppermute | solution.py:15
  27.8 7.1 %collective-permute-start.6 = (f32[4,16,2,128]{3,2,1,0:T(2,128)S(1)}, f32[4,16,2,128]{3,2,1,0:T(2,128)S(1)}, u32[]{:S(2)}, u32[]{:S(2)}) collective-permute-start(f32[4,16,2,128]{3,2,1,0:T(2,128)S(1)} %collective-permute-done.5), channel_id=1, source_target_pairs={{0,128},{8,136},{16,144},{24,152},{32,160},{40,168},{48,176},{56,1... | collective-permute-start | bytes 196616 | tf_op jit(solution)/shard_map/ppermute | solution.py:15
  34.9 0.0 collective-permute-done
  34.9 0.0 collective-permute-done.1
  34.9 2.6 %pad_maximum_fusion.3 = f32[4,16,132,128]{3,2,1,0:T(8,128)S(1)} fusion(f32[4,16,2,128]{3,2,1,0:T(2,128)S(1)} %collective-permute-done.1, f32[4,16,128,128]{3,2,1,0:T(8,128)} %copy-done.3, f32[4,16,2,128]{3,2,1,0:T(2,128)S(1)} %collective-permute-done), kind=kLoop, calls=%fused_computation.8 | loop fusion | flops 2162688 | bytes 8650752 | tf_op jit(solution)/shard_map/concatenate | solution.py:24
  37.5 0.3 collective-permute-done.6
  37.8 0.1 select_dynamic-update-slice_fusion
  37.9 0.0 copy-start
  37.9 4.9 %fusion.35 = (f32[4,16,132,2]{3,2,1,0:T(8,128)}, f32[4,16,132,2]{3,2,1,0:T(8,128)}) fusion(f32[4,16,132,128]{3,2,1,0:T(8,128)S(1)} %select_dynamic-update-slice_fusion), kind=kLoop, calls=%fused_computation.71 | loop fusion | bytes 270336 | tf_op jit(solution)/shard_map/slice | solution.py:23
  42.8 0.0 copy-done
  42.8 4.0 %copy.10 = f32[4,16,132,2]{2,1,3,0:T(8,128)S(1)} copy(f32[4,16,132,2]{3,2,1,0:T(8,128)} %get-tuple-element.23) | data formatting | bytes 135168 | tf_op jit(solution)/shard_map/slice | solution.py:22
  46.8 0.2 collective-permute-start.7
  47.0 4.0 %copy.12 = f32[4,16,132,2]{2,1,3,0:T(8,128)S(1)} copy(f32[4,16,132,2]{3,2,1,0:T(8,128)} %get-tuple-element.22) | data formatting | bytes 135168 | tf_op jit(solution)/shard_map/slice | solution.py:23
  51.1 0.6 collective-permute-start.8
  51.7 3.2 %slice_bitcast_fusion.7 = (f32[16,128,128]{2,1,0:T(8,128)}, f32[16,128,128]{2,1,0:T(8,128)}) fusion(f32[4,16,132,128]{3,2,1,0:T(8,128)} %copy-done), kind=kLoop, calls=%fused_computation.62 | loop fusion | bytes 4194304 | tf_op jit(solution)/shard_map/mul | solution.py:53
  54.8 0.0 collective-permute-done.7
  54.8 2.9 %copy.11 = f32[4,16,132,2]{3,2,1,0:T(8,128)} copy(f32[4,16,132,2]{2,1,3,0:T(8,128)S(1)} %collective-permute-done.7) | data formatting | bytes 135168 | tf_op jit(solution)/shard_map/ppermute | solution.py:28
  57.8 3.5 %collective-permute-done.8 = f32[4,16,132,2]{2,1,3,0:T(8,128)S(1)} collective-permute-done((f32[4,16,132,2]{2,1,3,0:T(8,128)S(1)}, f32[4,16,132,2]{2,1,3,0:T(8,128)S(1)}, u32[]{:S(2)}, u32[]{:S(2)}) %collective-permute-start.8) | collective-permute-done | bytes 67616 | tf_op jit(solution)/shard_map/ppermute | solution.py:26
  61.3 0.0 slice-start
  61.3 3.0 %copy.13 = f32[4,16,132,2]{3,2,1,0:T(8,128)} copy(f32[4,16,132,2]{2,1,3,0:T(8,128)S(1)} %collective-permute-done.8) | data formatting | bytes 135168 | tf_op jit(solution)/shard_map/ppermute | solution.py:26
  64.3 0.0 slice-start.1
  64.3 0.0 copy-start.1
  64.3 0.0 copy-start.2
  64.3 7.3 %pad_maximum_fusion.2 = f32[4,16,132,132]{3,2,1,0:T(8,128)S(1)} fusion(f32[4,16,132,2]{3,2,1,0:T(8,128)} %copy.11, f32[4,16,132,128]{3,2,1,0:T(8,128)} %copy-done, f32[4,16,132,2]{3,2,1,0:T(8,128)} %copy.13), kind=kLoop, calls=%fused_computation.7 | loop fusion | flops 2230272 | bytes 8921088 | tf_op jit(solution)/shard_map/concatenate | solution.py:24
  71.6 0.0 slice-done
  71.6 0.0 slice-done.1
  71.7 0.1 copy-done.1
  71.7 1.3 %copy-done.2 = f32[4,16,132,2]{3,2,1,0:T(8,128)S(1)} copy-done((f32[4,16,132,2]{3,2,1,0:T(8,128)S(1)}, f32[4,16,132,2]{3,2,1,0:T(8,128)}, u32[]{:S(2)}) %copy-start.2) | copy-done | bytes 67608
  73.0 11.3 %fusion = f32[4,16,130,130]{3,2,1,0:T(8,128)} fusion(f32[4,16,132,132]{3,2,1,0:T(8,128)S(1)} %pad_maximum_fusion.2, f32[4,16,132,128]{3,2,1,0:T(8,128)S(1)} %bitcast.67, f32[4,16,132,2]{3,2,1,0:T(8,128)S(1)} %copy-done.2, f32[4,16,132,2]{3,2,1,0:T(8,128)S(1)} %copy-done.1), kind=kLoop, calls=%fused_computation.1 | loop fusion | flops 7571200 | bytes 21766144 | tf_op jit(solution)/shard_map/sub | solution.py:37
  84.3 1.0 multiply_subtract_fusion
  85.4 18.4 %fusion.3 = f32[4,16,128,128]{3,2,1,0:T(8,128)} fusion(f32[4,16,130,130]{3,2,1,0:T(8,128)} %fusion), kind=kLoop, calls=%fused_computation.10 | loop fusion | flops 5242880 | bytes 25165824 | tf_op jit(solution)/shard_map/sub | solution.py:37
  103.8 0.0 copy-start.4
  103.8 7.9 %fusion.6 = f32[4,16,128,128]{3,2,1,0:T(8,128)} fusion(f32[4,16,132,128]{3,2,1,0:T(8,128)S(1)} %bitcast.67, f32[4,16,132,2]{3,2,1,0:T(8,128)} %copy.13, f32[4,16,132,2]{3,2,1,0:T(8,128)S(1)} %copy-done.1, f32[16,128,128]{2,1,0:T(8,128)} %get-tuple-element.21, f32[16,128,128]{2,1,0:T(8,128)} %get-tuple-element.20), kind=kLoop, calls=%fused_computation.17 | loop fusion | flops 8388608 | bytes 23660544 | tf_op jit(solution)/shard_map/mul | solution.py:53
  111.6 0.0 copy-done.4
  111.6 0.0 copy-start.5
  111.7 2.3 %fusion.28 = (f32[1,16,128,128]{3,2,1,0:T(8,128)S(1)}, f32[1,16,128,128]{3,2,1,0:T(8,128)S(1)}) fusion(f32[4,16,128,128]{3,2,1,0:T(8,128)S(1)} %copy-done.4, f32[4,16,128,128]{3,2,1,0:T(8,128)} %fusion.6, f32[4,16,132,128]{3,2,1,0:T(8,128)S(1)} %bitcast.67), kind=kLoop, calls=%fused_computation.58 | loop fusion | flops 2097152 | bytes 8388608 | tf_op jit(solution)/shard_map/sub | solution.py:57
  114.0 0.5 copy-done.5
  114.5 1.5 %fusion.20 = (f32[1,16,128,128]{3,2,1,0:T(8,128)S(1)}, f32[1,16,128,128]{3,2,1,0:T(8,128)S(1)}) fusion(f32[4,16,128,128]{3,2,1,0:T(8,128)S(1)} %copy-done.4, f32[4,16,128,128]{3,2,1,0:T(8,128)S(1)} %copy-done.5, f32[16,132,132]{2,1,0:T(8,128)S(1)} %multiply_subtract_fusion, f32[128]{0:T(128)S(1)} %get-tuple-element.30, f32[4,16,132,128]{3,2,1,0:T(8,128)S(1)} %bitcast.67, ...), kind=kLoop, calls=%fused_computation.45 | loop fusion | flops 4718592 | bytes 12583936 | tf_op jit(solution)/shard_map/stack | solution.py:65
  116.0 0.4 maximum_multiply_fusion.1
  116.4 2.1 %slice_bitcast_fusion = (f32[16,128,128]{2,1,0:T(8,128)}, f32[16,128,128]{2,1,0:T(8,128)}, f32[16,128,128]{2,1,0:T(8,128)}, f32[16,128,128]{2,1,0:T(8,128)}) fusion(f32[4,16,128,128]{3,2,1,0:T(8,128)S(1)} %maximum_multiply_fusion.1), kind=kLoop, calls=%fused_computation.27 | loop fusion | bytes 8388608 | tf_op jit(solution)/shard_map/squeeze | solution.py:96
  (3 shorter events, 0.1 us)
Async XLA Ops:
  1.6 4.9 %copy-start.6 = (f32[4]{0:T(128)S(1)}, f32[4]{0:T(128)}, u32[]{:S(2)}) copy-start(f32[4]{0:T(128)} %constant.71.clone) | copy-start | bytes 52
  4.2 1.9 %copy-start.3 = (f32[4,16,128,128]{3,2,1,0:T(8,128)}, f32[4,16,128,128]{3,2,1,0:T(8,128)S(1)}, u32[]{:S(2)}) copy-start(f32[4,16,128,128]{3,2,1,0:T(8,128)S(1)} %maximum_multiply_fusion) | copy-start | bytes 12582916
  6.6 1.3 %collective-permute-start.2 = (f32[4,16,2,128]{3,2,1,0:T(2,128)S(1)}, f32[4,16,2,128]{3,2,1,0:T(2,128)S(1)}, u32[]{:S(2)}, u32[]{:S(2)}) collective-permute-start(f32[4,16,2,128]{3,2,1,0:T(2,128)S(1)} %broadcast_multiply_fusion), channel_id=1, source_target_pairs={{0,8},{8,0},{16,24},{24,16},{32,40},{40,32},{48,56},{56,48},{64,72... | collective-permute-start | bytes 196616 | tf_op jit(solution)/shard_map/ppermute | solution.py:15
  7.9 4.3 %collective-permute-start.3 = (f32[4,16,2,128]{3,2,1,0:T(2,128)S(1)}, f32[4,16,2,128]{3,2,1,0:T(2,128)S(1)}, u32[]{:S(2)}, u32[]{:S(2)}) collective-permute-start(f32[4,16,2,128]{3,2,1,0:T(2,128)S(1)} %collective-permute-done.2), channel_id=1, source_target_pairs={{0,16},{8,24},{16,0},{24,8},{32,48},{40,56},{48,32},{56,40},{64,80... | collective-permute-start | bytes 196616 | tf_op jit(solution)/shard_map/ppermute | solution.py:15
  12.2 9.9 %collective-permute-start.4 = (f32[4,16,2,128]{3,2,1,0:T(2,128)S(1)}, f32[4,16,2,128]{3,2,1,0:T(2,128)S(1)}, u32[]{:S(2)}, u32[]{:S(2)}) collective-permute-start(f32[4,16,2,128]{3,2,1,0:T(2,128)S(1)} %collective-permute-done.3), channel_id=1, source_target_pairs={{0,32},{8,40},{16,48},{24,56},{32,0},{40,8},{48,16},{56,24},{64,96... | collective-permute-start | bytes 196616 | tf_op jit(solution)/shard_map/ppermute | solution.py:15
  15.4 19.5 %collective-permute-start = (f32[4,16,2,128]{3,2,1,0:T(2,128)S(1)}, f32[4,16,2,128]{3,2,1,0:T(2,128)S(1)}, u32[]{:S(2)}, u32[]{:S(2)}) collective-permute-start(f32[4,16,2,128]{3,2,1,0:T(2,128)S(1)} %get-tuple-element.28), channel_id=1, source_target_pairs={{0,1},{1,2},{2,3},{3,4},{4,5},{5,6},{6,7},{8,9},{9,10},{10,11},{11... | collective-permute-start | bytes 196616 | tf_op jit(solution)/shard_map/ppermute | solution.py:26
  19.2 15.7 %collective-permute-start.1 = (f32[4,16,2,128]{3,2,1,0:T(2,128)S(1)}, f32[4,16,2,128]{3,2,1,0:T(2,128)S(1)}, u32[]{:S(2)}, u32[]{:S(2)}) collective-permute-start(f32[4,16,2,128]{3,2,1,0:T(2,128)S(1)} %get-tuple-element.29), channel_id=1, source_target_pairs={{1,0},{2,1},{3,2},{4,3},{5,4},{6,5},{7,6},{9,8},{10,9},{11,10},{12... | collective-permute-start | bytes 196616 | tf_op jit(solution)/shard_map/ppermute | solution.py:28
  22.2 5.6 %collective-permute-start.5 = (f32[4,16,2,128]{3,2,1,0:T(2,128)S(1)}, f32[4,16,2,128]{3,2,1,0:T(2,128)S(1)}, u32[]{:S(2)}, u32[]{:S(2)}) collective-permute-start(f32[4,16,2,128]{3,2,1,0:T(2,128)S(1)} %collective-permute-done.4), channel_id=1, source_target_pairs={{0,64},{8,72},{16,80},{24,88},{32,96},{40,104},{48,112},{56,120},{... | collective-permute-start | bytes 196616 | tf_op jit(solution)/shard_map/ppermute | solution.py:15
  27.8 10.1 %collective-permute-start.6 = (f32[4,16,2,128]{3,2,1,0:T(2,128)S(1)}, f32[4,16,2,128]{3,2,1,0:T(2,128)S(1)}, u32[]{:S(2)}, u32[]{:S(2)}) collective-permute-start(f32[4,16,2,128]{3,2,1,0:T(2,128)S(1)} %collective-permute-done.5), channel_id=1, source_target_pairs={{0,128},{8,136},{16,144},{24,152},{32,160},{40,168},{48,176},{56,1... | collective-permute-start | bytes 196616 | tf_op jit(solution)/shard_map/ppermute | solution.py:15
  37.9 4.9 %copy-start = (f32[4,16,132,128]{3,2,1,0:T(8,128)}, f32[4,16,132,128]{3,2,1,0:T(8,128)S(1)}, u32[]{:S(2)}) copy-start(f32[4,16,132,128]{3,2,1,0:T(8,128)S(1)} %select_dynamic-update-slice_fusion) | copy-start | bytes 12976132
  46.8 8.0 %collective-permute-start.7 = (f32[4,16,132,2]{2,1,3,0:T(8,128)S(1)}, f32[4,16,132,2]{2,1,3,0:T(8,128)S(1)}, u32[]{:S(2)}, u32[]{:S(2)}) collective-permute-start(f32[4,16,132,2]{2,1,3,0:T(8,128)S(1)} %copy.10), channel_id=1, source_target_pairs={{8,0},{16,8},{24,16},{32,24},{40,32},{48,40},{56,48},{64,56},{72,6... | collective-permute-start | bytes 202760 | tf_op jit(solution)/shard_map/ppermute | solution.py:28
  51.1 10.3 %collective-permute-start.8 = (f32[4,16,132,2]{2,1,3,0:T(8,128)S(1)}, f32[4,16,132,2]{2,1,3,0:T(8,128)S(1)}, u32[]{:S(2)}, u32[]{:S(2)}) collective-permute-start(f32[4,16,132,2]{2,1,3,0:T(8,128)S(1)} %copy.12), channel_id=1, source_target_pairs={{0,8},{8,16},{16,24},{24,32},{32,40},{40,48},{48,56},{56,64},{64,7... | collective-permute-start | bytes 202760 | tf_op jit(solution)/shard_map/ppermute | solution.py:26
  61.3 10.3 %slice-start = ((s8[4456448]{0:T(1024)(128)(4,1)}), s8[262144]{0:T(1024)(128)(4,1)S(1)}, s32[]{:S(2)}) async-start(s8[4456448]{0:T(1024)(128)(4,1)} %bitcast.66), calls=%async_computation | async-start | bytes 524288
  64.3 7.3 %slice-start.1 = ((s8[4456448]{0:T(1024)(128)(4,1)}), s8[4194304]{0:T(1024)(128)(4,1)S(1)}, s32[]{:S(2)}) async-start(s8[4456448]{0:T(1024)(128)(4,1)} %bitcast.66), calls=%async_computation.1 | async-start | bytes 8388608
  64.3 7.4 %copy-start.1 = (f32[4,16,132,2]{3,2,1,0:T(8,128)S(1)}, f32[4,16,132,2]{3,2,1,0:T(8,128)}, u32[]{:S(2)}) copy-start(f32[4,16,132,2]{3,2,1,0:T(8,128)} %copy.11) | copy-start | bytes 202756
  64.3 8.7 %copy-start.2 = (f32[4,16,132,2]{3,2,1,0:T(8,128)S(1)}, f32[4,16,132,2]{3,2,1,0:T(8,128)}, u32[]{:S(2)}) copy-start(f32[4,16,132,2]{3,2,1,0:T(8,128)} %copy.13) | copy-start | bytes 202756
  103.8 7.9 %copy-start.4 = (f32[4,16,128,128]{3,2,1,0:T(8,128)S(1)}, f32[4,16,128,128]{3,2,1,0:T(8,128)}, u32[]{:S(2)}) copy-start(f32[4,16,128,128]{3,2,1,0:T(8,128)} %fusion.3) | copy-start | bytes 12582916
  111.6 2.8 %copy-start.5 = (f32[4,16,128,128]{3,2,1,0:T(8,128)S(1)}, f32[4,16,128,128]{3,2,1,0:T(8,128)}, u32[]{:S(2)}) copy-start(f32[4,16,128,128]{3,2,1,0:T(8,128)} %fusion.6) | copy-start | bytes 12582916
where the time goes:
time: 119 us; the launch traced here: 118 us
  other arithmetic  56.5 us (47%)
  local copies, waits for them, and re-layouts  28.3 us (24%)
  starting transfers between devices  22.9 us (19%)
  waiting for transfers between devices  10 us (8%)
    sub x2, other arithmetic, laplace(): grid[..., 2:, 1:-1] + grid[..., :-2, 1:-1] + grid[..., 1:-1, 2:]  29.7 us
    ppermute x5, starting transfers between devices, from_partner(): return lax.ppermute(value, axis, pairs)  15.3 us
    concatenate x2, other arithmetic, padded(): jnp.concatenate([lax.ppermute(tail, axis, [(i, (i + 1) % count) for i in...  9.91 us
    slice x3, local copies, waits for them, and re-layouts, padded(): lax.slice_in_dim(cells, cells.shape[dim] - width, cells.shape[dim], axis=...  8.97 us
    mul x1, other arithmetic, advance(): carried = 0.5 * (first * (east - west) + second * (north - south))  7.86 us
    ppermute x5, waiting for transfers between devices, from_partner(): return lax.ppermute(value, axis, pairs)  6.45 us
    ppermute x2, starting transfers between devices, padded(): lax.ppermute(tail, axis, [(i, (i + 1) % count) for i in range(ends)])  4.44 us
    slice x1, local copies, waits for them, and re-layouts, padded(): head = lax.slice_in_dim(cells, 0, width, axis=dim)  4.03 us
  transfers between devices with their start and end apart: 9, of which 5 were waited for; matrix products, arithmetic and copies ran while one was open for 11% of the time, Pallas kernels for 0%

commit v1 on v0

v1 whole, which is shorter than its diff:
```python
import math

import jax
import jax.numpy as jnp
from jax import lax
from jax.experimental import pallas as pl
from jax.experimental.pallas import tpu as pltpu
from jax.sharding import PartitionSpec as P

time_step = 0.2
biharmonic = 0.01
signs = (1.0, 1.0, -1.0, -1.0)
top = 8


def step_kernel(t_ref, s_ref, u_ref, v_ref, d_ref, f_ref, rs_ref, rn_ref, cw_ref, ce_ref,
                to_ref, so_ref, uo_ref, vo_ref,
                base, vp1, vm1, vp2, vm2, accx, accy):
    k = pl.program_id(0)
    frame, width = base.shape[1], base.shape[2]
    rows = t_ref.shape[1]

    @pl.when(k == 0)
    def _():
        base[...] = jnp.zeros_like(base)
        accx[...] = jnp.zeros_like(accx)
        accy[...] = jnp.zeros_like(accy)

    wet = jnp.where(d_ref[...] > k, 1.0, 0.0).astype(jnp.float32)
    lane = lax.broadcasted_iota(jnp.int32, (frame, width), 1)
    ins = (t_ref, s_ref, u_ref, v_ref)
    for n in range(4):
        base[n, top:top + rows, :] = ins[n][0] * wet
        base[n, top - 2:top, :] = rs_ref[n, 0]
        base[n, top + rows:top + rows + 2, :] = rn_ref[n, 0]
        whole = base[n]
        ce = ce_ref[n, 0]
        cw = cw_ref[n, 0]
        e0 = jnp.broadcast_to(ce[:, 0:1], (frame, width))
        e1 = jnp.broadcast_to(ce[:, 1:2], (frame, width))
        w0 = jnp.broadcast_to(cw[:, 0:1], (frame, width))
        w1 = jnp.broadcast_to(cw[:, 1:2], (frame, width))
        vp1[n] = jnp.where(lane == width - 1, e0, pltpu.roll(whole, width - 1, 1))
        vm1[n] = jnp.where(lane == 0, w1, pltpu.roll(whole, 1, 1))
        vp2[n] = jnp.where(lane == width - 2, e0,
                           jnp.where(lane == width - 1, e1, pltpu.roll(whole, width - 2, 1)))
        vm2[n] = jnp.where(lane == 0, w0, jnp.where(lane == 1, w1, pltpu.roll(whole, 2, 1)))

    def at(ref, n, d):
        return ref[n, top + d:top + d + rows, :]

    centre = [at(base, n, 0) for n in range(4)]
    first, second = centre[2], centre[3]
    parts = []
    for n in range(4):
        east, west = at(vp1, n, 0), at(vm1, n, 0)
        north, south = at(base, n, 1), at(base, n, -1)
        carried = 0.5 * (first * (east - west) + second * (north - south))
        smooth = (
            20.0 * centre[n]
            - 8.0 * (east + west + north + south)
            + 2.0 * (at(vp1, n, 1) + at(vp1, n, -1) + at(vm1, n, 1) + at(vm1, n, -1))
            + at(base, n, 2) + at(base, n, -2) + at(vp2, n, 0) + at(vm2, n, 0)
        )
        parts.append((east, west, north, south, carried, smooth))

    def density(a, b):
        return -0.2 * a + 0.8 * b

    dx = density(parts[0][0], parts[1][0]) - density(parts[0][1], parts[1][1])
    dy = density(parts[0][2], parts[1][2]) - density(parts[0][3], parts[1][3])
    totx = accx[...] + dx
    toty = accy[...] + dy
    accx[...] = totx
    accy[...] = toty
    grad_x = 0.5 * (totx - 0.5 * dx)
    grad_y = 0.5 * (toty - 0.5 * dy)
    coriolis = f_ref[...]
    to_ref[0] = (centre[0] - time_step * parts[0][4] - biharmonic * parts[0][5]) * wet
    so_ref[0] = (centre[1] - time_step * parts[1][4] - biharmonic * parts[1][5]) * wet
    uo_ref[0] = (
        first + time_step * (coriolis * second - grad_x - parts[2][4]) - biharmonic * parts[2][5]
    ) * wet
    vo_ref[0] = (
        second + time_step * (-coriolis * first - grad_y - parts[3][4]) - biharmonic * parts[3][5]
    ) * wet


def shards(temp, salt, uvel, vvel, depth_levels):
    levels, rows_dev, cols_dev = temp.shape
    nlat = lax.axis_size("lat")
    nlon = lax.axis_size("lon")
    at_lat = lax.axis_index("lat")
    fields = (temp, salt, uvel, vvel)
    level_index = jnp.arange(levels, dtype=jnp.int32)[:, None, None]

    def masked_rows(lo, hi):
        wet = jnp.where(depth_levels[None, lo:hi, :] > level_index, 1.0, 0.0).astype(jnp.float32)
        return jnp.stack([x[:, lo:hi, :] * wet for x in fields])

    def masked_cols(lo, hi):
        wet = jnp.where(depth_levels[None, :, lo:hi] > level_index, 1.0, 0.0).astype(jnp.float32)
        return jnp.stack([x[:, :, lo:hi] * wet for x in fields])

    head = masked_rows(0, 2)
    tail = masked_rows(rows_dev - 2, rows_dev)
    south = lax.ppermute(tail, "lat", [(i, i + 1) for i in range(nlat - 1)])
    north = lax.ppermute(head, "lat", [(i + 1, i) for i in range(nlat - 1)])
    sign = jnp.array(signs, jnp.float32)[:, None, None, None]
    piece = tail[:, :, ::-1, ::-1] * sign
    last = nlat - 1
    fold = lax.ppermute(
        piece, ("lon", "lat"), [(i * nlat + last, (nlon - 1 - i) * nlat + last) for i in range(nlon)]
    )
    north = north + fold

    pad = top - 2
    frame = rows_dev + 2 * top

    def strip(lo, hi):
        zeros = jnp.zeros((4, levels, pad, hi - lo), jnp.float32)
        return jnp.concatenate(
            [zeros, south[..., lo:hi], masked_cols(lo, hi), north[..., lo:hi], zeros], axis=2
        )

    west = lax.ppermute(
        strip(cols_dev - 2, cols_dev), "lon", [(i, (i + 1) % nlon) for i in range(nlon)]
    )
    east = lax.ppermute(strip(0, 2), "lon", [((i + 1) % nlon, i) for i in range(nlon)])

    total_rows = rows_dev * nlat
    global_rows = (at_lat * rows_dev + jnp.arange(rows_dev, dtype=jnp.int32)).astype(jnp.float32)
    coriolis = (0.5 * jnp.sin(math.pi * (global_rows + 0.5) / total_rows - 0.5 * math.pi))[:, None]
    coriolis = jnp.broadcast_to(coriolis, (rows_dev, cols_dev))

    level_block = pl.BlockSpec((1, rows_dev, cols_dev), lambda k: (k, 0, 0))
    plane = pl.BlockSpec((rows_dev, cols_dev), lambda k: (0, 0))
    row_halo = pl.BlockSpec((4, 1, 2, cols_dev), lambda k: (0, k, 0, 0))
    col_halo = pl.BlockSpec((4, 1, frame, 2), lambda k: (0, k, 0, 0))
    out = pl.pallas_call(
        step_kernel,
        grid=(levels,),
        in_specs=[level_block] * 4 + [plane] * 2 + [row_halo] * 2 + [col_halo] * 2,
        out_specs=[level_block] * 4,
        out_shape=[jax.ShapeDtypeStruct(temp.shape, jnp.float32)] * 4,
        scratch_shapes=[pltpu.VMEM((4, frame, cols_dev), jnp.float32)] * 5
        + [pltpu.VMEM((rows_dev, cols_dev), jnp.float32)] * 2,
        compiler_params=pltpu.CompilerParams(dimension_semantics=("arbitrary",)),
    )(temp, salt, uvel, vvel, depth_levels, coriolis, south, north, west, east)
    return tuple(out)


def solution(mesh):
    placed = (
        P(None, "lat", "lon"),
        P(None, "lat", "lon"),
        P(None, "lat", "lon"),
        P(None, "lat", "lon"),
        P("lat", "lon"),
    )
    return jax.shard_map(
        shards,
        mesh=mesh,
        in_specs=placed,
        out_specs=(
            P(None, "lat", "lon"),
            P(None, "lat", "lon"),
            P(None, "lat", "lon"),
            P(None, "lat", "lon"),
        ),
        check_vma=False,
    )
```

time: 119 us -> 72.4 us (0.61)
  the two profiles are of different devices: /device:TPU:4 before, /device:TPU:91 now
where the time goes in v1:
time: 72.4 us; the launch traced here: 71.6 us
  local copies, waits for them, and re-layouts  27.5 us (38%)
  Pallas kernels  18.4 us (25%)
  starting transfers between devices  12 us (17%)
  waiting for transfers between devices  9.55 us (13%)
  other arithmetic  3.4 us (5%)
  between operations  0.81 us (1%)
    pallas_call x1, Pallas kernels, shards(): pl.pallas_call(step_kernel, grid=(levels,), in_specs=[level_block] * 4 +...  18.4 us
    ppermute x1, waiting for transfers between devices, shards(): lax.ppermute(strip(0, 2), 'lon', [((i + 1) % nlon, i) for i in range(nlon)])  9.54 us
    unnamed x20, local copies, waits for them, and re-layouts  8.97 us
    slice x4, local copies, waits for them, and re-layouts, masked_cols(): return jnp.stack([x[:, :, lo:hi] * wet for x in fields])  6.9 us
    ppermute x1, starting transfers between devices, shards(): lax.ppermute(strip(cols_dev - 2, cols_dev), 'lon', [(i, (i + 1) % nlon) f...  5.06 us
    ppermute x1, starting transfers between devices, shards(): south = lax.ppermute(tail, 'lat', [(i, i + 1) for i in range(nlat - 1)])  3.55 us
    ppermute x1, local copies, waits for them, and re-layouts, shards(): lax.ppermute(strip(0, 2), 'lon', [((i + 1) % nlon, i) for i in range(nlon)])  3.1 us
    ppermute x1, local copies, waits for them, and re-layouts, shards(): lax.ppermute(strip(cols_dev - 2, cols_dev), 'lon', [(i, (i + 1) % nlon) f...  3.06 us
  transfers between devices with their start and end apart: 5, of which 1 were waited for; matrix products, arithmetic and copies ran while one was open for 33% of the time, Pallas kernels for 0%

profile of v1, /device:TPU:91, one launch (start us, length us, event | category | flops | bytes accessed | tf_op | source)
XLA Modules:
  0.0 71.6 jit_solution(9487113383191357789)
XLA Ops:
  0.6 0.0 copy-start
  0.6 0.8 %fusion.15 = (s32[2,128]{1,0:T(2,128)S(1)}, s32[2,128]{1,0:T(2,128)S(1)}) fusion(s32[128,128]{1,0:T(8,128)} %d_ref.1), kind=kLoop, calls=%fused_computation.41 | loop fusion | bytes 4096 | tf_op jit(solution)/shard_map/slice | solution.py:98
  1.4 0.0 copy-start.1
  1.4 1.2 %multiply_bitcast_fusion = (f32[1,16,2,128]{3,2,1,0:T(2,128)S(1)}, f32[1,16,2,128]{3,2,1,0:T(2,128)S(1)}, f32[1,16,2,128]{3,2,1,0:T(2,128)S(1)}, f32[1,16,2,128]...) fusion(f32[16,128,128]{2,1,0:T(8,128)} %v_ref.1, ...), kind=kLoop, calls=%fused_computation.25 | loop fusion | flops 49152 | bytes 264192 | tf_op jit(solution)/shard_map/stack | solution.py:99
  2.7 3.5 %collective-permute-start = (f32[4,16,2,128]{3,2,1,0:T(2,128)S(1)}, f32[4,16,2,128]{3,2,1,0:T(2,128)S(1)}, u32[]{:S(2)}, u32[]{:S(2)}) collective-permute-start(f32[4,16,2,128]{3,2,1,0:T(2,128)S(1)} %pad_maximum_fusion), channel_id=1, source_target_pairs={{0,1},{1,2},{2,3},{3,4},{4,5},{5,6},{6,7},{8,9},{9,10},{10,11},{11... | collective-permute-start | bytes 196616 | tf_op jit(solution)/shard_map/ppermute | solution.py:107
  6.3 0.3 rev.3
  6.6 1.4 %broadcast_multiply_fusion = f32[4,16,2,128]{3,2,1,0:T(2,128)} fusion(f32[4,16,2,128]{3,2,1,0:T(2,128)S(1)} %rev.3, f32[4]{0:T(128)} %constant.23.clone), kind=kLoop, calls=%fused_computation.4 | loop fusion | flops 16384 | bytes 131088 | tf_op jit(solution)/shard_map/mul | solution.py:110
  7.9 0.7 collective-permute-start.2
  8.6 0.6 pad_maximum_fusion.1
  9.2 2.6 %collective-permute-start.1 = (f32[4,16,2,128]{3,2,1,0:T(2,128)}, f32[4,16,2,128]{3,2,1,0:T(2,128)S(1)}, u32[]{:S(2)}, u32[]{:S(2)}) collective-permute-start(f32[4,16,2,128]{3,2,1,0:T(2,128)} %pad_maximum_fusion.1), channel_id=1, source_target_pairs={{1,0},{2,1},{3,2},{4,3},{5,4},{6,5},{7,6},{9,8},{10,9},{11,10},{12... | collective-permute-start | bytes 196616 | tf_op jit(solution)/shard_map/ppermute | solution.py:108
  11.9 1.0 %fusion.13 = (s32[128,2]{1,0:T(8,128)S(1)}, s32[128,2]{1,0:T(8,128)S(1)}) fusion(s32[128,128]{1,0:T(8,128)} %d_ref.1), kind=kLoop, calls=%fused_computation.39 | loop fusion | bytes 4096 | tf_op jit(solution)/shard_map/slice | solution.py:102
  12.9 3.2 %fusion.8 = (f32[16,128,2]{2,1,0:T(8,128)}, f32[16,128,2]{2,1,0:T(8,128)}) fusion(f32[16,128,128]{2,1,0:T(8,128)} %t_ref.1), kind=kLoop, calls=%fused_computation.34 | loop fusion | bytes 65536 | tf_op jit(solution)/shard_map/slice | solution.py:103
  16.1 0.0 copy-done
  16.1 0.0 copy-start.2
  16.1 1.7 %fusion.9 = (f32[16,128,2]{2,1,0:T(8,128)}, f32[16,128,2]{2,1,0:T(8,128)}) fusion(f32[16,128,128]{2,1,0:T(8,128)S(1)} %copy-done), kind=kLoop, calls=%fused_computation.35 | loop fusion | bytes 65536 | tf_op jit(solution)/shard_map/slice | solution.py:103
  17.7 0.0 copy-done.1
  17.7 1.7 %fusion.10 = (f32[16,128,2]{2,1,0:T(8,128)}, f32[16,128,2]{2,1,0:T(8,128)}) fusion(f32[16,128,128]{2,1,0:T(8,128)S(1)} %copy-done.1), kind=kLoop, calls=%fused_computation.36 | loop fusion | bytes 65536 | tf_op jit(solution)/shard_map/slice | solution.py:103
  19.4 0.0 copy-done.2
  19.4 0.4 fusion.11
  19.8 0.0 copy-start.3
  19.8 0.1 copy.18
  19.9 0.1 copy.11
  19.9 1.7 %copy.30 = f32[16,128,2]{1,0,2:T(8,128)S(1)} copy(f32[16,128,2]{2,1,0:T(8,128)} %get-tuple-element.4) | data formatting | bytes 32768
  21.6 1.6 %copy.26 = f32[16,128,2]{1,0,2:T(8,128)S(1)} copy(f32[16,128,2]{2,1,0:T(8,128)} %get-tuple-element.5) | data formatting | bytes 32768
  23.2 1.6 %copy.31 = f32[16,128,2]{1,0,2:T(8,128)S(1)} copy(f32[16,128,2]{2,1,0:T(8,128)} %get-tuple-element.6) | data formatting | bytes 32768
  24.7 1.6 %copy.27 = f32[16,128,2]{1,0,2:T(8,128)S(1)} copy(f32[16,128,2]{2,1,0:T(8,128)} %get-tuple-element.7) | data formatting | bytes 32768
  26.3 1.6 %copy.32 = f32[16,128,2]{1,0,2:T(8,128)S(1)} copy(f32[16,128,2]{2,1,0:T(8,128)} %get-tuple-element.8) | data formatting | bytes 32768
  27.9 0.0 copy-done.3
  27.9 0.3 copy.28
  28.2 0.3 copy.33
  28.5 0.3 copy.29
  29.0 0.0 collective-permute-done.2
  29.0 0.0 collective-permute-done.1
  29.0 0.0 copy-start.4
  29.0 0.1 fusion.12
  29.2 0.5 copy.23
  29.7 0.5 copy.16
  30.1 0.0 collective-permute-done.rs_ref
  30.2 0.0 copy-start.5
  30.2 0.1 fusion.14
  30.3 0.5 copy.22
  30.8 0.5 copy.15
  31.3 0.2 concatenate.6
  31.4 5.1 %collective-permute-start.3 = (f32[4,16,144,2]{2,1,3,0:T(8,128)S(1)}, f32[4,16,144,2]{2,1,3,0:T(8,128)S(1)}, u32[]{:S(2)}, u32[]{:S(2)}) collective-permute-start(f32[4,16,144,2]{2,1,3,0:T(8,128)S(1)} %concatenate.6), channel_id=1, source_target_pairs={{0,8},{8,16},{16,24},{24,32},{32,40},{40,48},{48,56},{56,64},{64,7... | collective-permute-start | bytes 221192 | tf_op jit(solution)/shard_map/ppermute | solution.py:126
  36.5 0.1 concatenate.7
  36.7 0.1 collective-permute-start.4
  36.8 9.5 %collective-permute-done.4 = f32[4,16,144,2]{2,1,3,0:T(8,128)S(1)} collective-permute-done((f32[4,16,144,2]{2,1,3,0:T(8,128)S(1)}, f32[4,16,144,2]{2,1,3,0:T(8,128)S(1)}, u32[]{:S(2)}, u32[]{:S(2)}) %collective-permute-start.4) | collective-permute-done | bytes 73760 | tf_op jit(solution)/shard_map/ppermute | solution.py:129
  46.3 3.1 %copy.25.ce_ref = f32[4,16,144,2]{3,2,1,0:T(8,128)} copy(f32[4,16,144,2]{2,1,3,0:T(8,128)S(1)} %collective-permute-done.4) | data formatting | bytes 147456 | tf_op jit(solution)/shard_map/ppermute | solution.py:129
  49.4 0.0 collective-permute-done.3
  49.4 3.1 %copy.24.cw_ref = f32[4,16,144,2]{3,2,1,0:T(8,128)} copy(f32[4,16,144,2]{2,1,3,0:T(8,128)S(1)} %collective-permute-done.3) | data formatting | bytes 147456 | tf_op jit(solution)/shard_map/ppermute | solution.py:126
  52.5 0.0 copy-done.4
  52.5 0.0 copy-done.5
  52.5 0.7 broadcast_in_dim.32.f_ref
  53.2 18.4 %shard_map.93 = (f32[16,128,128]{2,1,0:T(8,128)}, f32[16,128,128]{2,1,0:T(8,128)}, f32[16,128,128]{2,1,0:T(8,128)}, f32[16,128,128]{2,1,0:T(8,128)}) custom-call(f32[16,128,128]{2,1,0:T(8,128)} %t_ref.1, f32[16,128,128]{2,1,0:T(8,128)} %s_ref.1, f32[16,128,128]{2,1,0:T(8,128)} %u_ref.1, f32[16,128,128]{2,1,0:T(8,128)} %v_ref.1, s32[128,128]{1,0:T(8,128)} %d_ref.1, ...), custom_call_target="tpu_custom_call" | custom-call | tf_op jit(solution)/shard_map/pallas_call | solution.py:140
  (8 shorter events, 0.2 us)
Async XLA Ops:
  0.6 15.4 %copy-start = (f32[16,128,128]{2,1,0:T(8,128)S(1)}, f32[16,128,128]{2,1,0:T(8,128)}, u32[]{:S(2)}) copy-start(f32[16,128,128]{2,1,0:T(8,128)} %s_ref.1) | copy-start | bytes 3145732
  1.4 16.3 %copy-start.1 = (f32[16,128,128]{2,1,0:T(8,128)S(1)}, f32[16,128,128]{2,1,0:T(8,128)}, u32[]{:S(2)}) copy-start(f32[16,128,128]{2,1,0:T(8,128)} %u_ref.1) | copy-start | bytes 3145732
  2.7 27.4 %collective-permute-start = (f32[4,16,2,128]{3,2,1,0:T(2,128)S(1)}, f32[4,16,2,128]{3,2,1,0:T(2,128)S(1)}, u32[]{:S(2)}, u32[]{:S(2)}) collective-permute-start(f32[4,16,2,128]{3,2,1,0:T(2,128)S(1)} %pad_maximum_fusion), channel_id=1, source_target_pairs={{0,1},{1,2},{2,3},{3,4},{4,5},{5,6},{6,7},{8,9},{9,10},{10,11},{11... | collective-permute-start | bytes 196616 | tf_op jit(solution)/shard_map/ppermute | solution.py:107
  7.9 21.0 %collective-permute-start.2 = (f32[4,16,2,128]{3,2,1,0:T(2,128)}, f32[4,16,2,128]{3,2,1,0:T(2,128)S(1)}, u32[]{:S(2)}, u32[]{:S(2)}) collective-permute-start(f32[4,16,2,128]{3,2,1,0:T(2,128)} %broadcast_multiply_fusion), channel_id=1, source_target_pairs={{7,255},{15,247},{23,239},{31,231},{39,223},{47,215},{55,207},{63,... | collective-permute-start | bytes 196616 | tf_op jit(solution)/shard_map/ppermute | solution.py:112
  9.2 19.7 %collective-permute-start.1 = (f32[4,16,2,128]{3,2,1,0:T(2,128)}, f32[4,16,2,128]{3,2,1,0:T(2,128)S(1)}, u32[]{:S(2)}, u32[]{:S(2)}) collective-permute-start(f32[4,16,2,128]{3,2,1,0:T(2,128)} %pad_maximum_fusion.1), channel_id=1, source_target_pairs={{1,0},{2,1},{3,2},{4,3},{5,4},{6,5},{7,6},{9,8},{10,9},{11,10},{12... | collective-permute-start | bytes 196616 | tf_op jit(solution)/shard_map/ppermute | solution.py:108
  16.1 3.3 %copy-start.2 = (f32[16,128,128]{2,1,0:T(8,128)S(1)}, f32[16,128,128]{2,1,0:T(8,128)}, u32[]{:S(2)}) copy-start(f32[16,128,128]{2,1,0:T(8,128)} %v_ref.1) | copy-start | bytes 3145732
  19.8 8.1 %copy-start.3 = (f32[16,128,2]{2,1,0:T(8,128)S(1)}, f32[16,128,2]{2,1,0:T(8,128)}, u32[]{:S(2)}) copy-start(f32[16,128,2]{2,1,0:T(8,128)} %get-tuple-element.9) | copy-start | bytes 49156
  29.0 23.5 %copy-start.4 = (f32[4,16,2,128]{3,2,1,0:T(2,128)}, f32[4,16,2,128]{3,2,1,0:T(2,128)S(1)}, u32[]{:S(2)}) copy-start(f32[4,16,2,128]{3,2,1,0:T(2,128)S(1)} %add.28.rn_ref) | copy-start | bytes 196612
  30.2 22.4 %copy-start.5 = (f32[4,16,2,128]{3,2,1,0:T(2,128)}, f32[4,16,2,128]{3,2,1,0:T(2,128)S(1)}, u32[]{:S(2)}) copy-start(f32[4,16,2,128]{3,2,1,0:T(2,128)S(1)} %collective-permute-done.rs_ref) | copy-start | bytes 196612
  31.4 18.0 %collective-permute-start.3 = (f32[4,16,144,2]{2,1,3,0:T(8,128)S(1)}, f32[4,16,144,2]{2,1,3,0:T(8,128)S(1)}, u32[]{:S(2)}, u32[]{:S(2)}) collective-permute-start(f32[4,16,144,2]{2,1,3,0:T(8,128)S(1)} %concatenate.6), channel_id=1, source_target_pairs={{0,8},{8,16},{16,24},{24,32},{32,40},{40,48},{48,56},{56,64},{64,7... | collective-permute-start | bytes 221192 | tf_op jit(solution)/shard_map/ppermute | solution.py:126
  36.7 9.7 %collective-permute-start.4 = (f32[4,16,144,2]{2,1,3,0:T(8,128)S(1)}, f32[4,16,144,2]{2,1,3,0:T(8,128)S(1)}, u32[]{:S(2)}, u32[]{:S(2)}) collective-permute-start(f32[4,16,144,2]{2,1,3,0:T(8,128)S(1)} %concatenate.7), channel_id=1, source_target_pairs={{8,0},{16,8},{24,16},{32,24},{40,32},{48,40},{56,48},{64,56},{72,6... | collective-permute-start | bytes 221192 | tf_op jit(solution)/shard_map/ppermute | solution.py:129

commit v2 on v1

v2 whole, which is shorter than its diff:
```python
import functools
import math

import jax
import jax.numpy as jnp
from jax import lax
from jax.experimental import pallas as pl
from jax.experimental.pallas import tpu as pltpu
from jax.sharding import PartitionSpec as P

time_step = 0.2
biharmonic = 0.01
signs = (1.0, 1.0, -1.0, -1.0)
top = 8


def when(cond, fn):
    if cond is True:
        fn()
    else:
        pl.when(cond)(fn)


def reverse_lanes(x):
    lane = lax.broadcasted_iota(jnp.int32, x.shape, 1)
    width = x.shape[1]
    bit = 1
    while bit < width:
        x = jnp.where((lane & bit) != 0, pltpu.roll(x, bit, 1), pltpu.roll(x, width - bit, 1))
        bit *= 2
    return x


def exchange_kernel(axes, nlat, nlon, t_ref, s_ref, u_ref, v_ref, d_ref,
                    hs_o, hn_o, hw_o, he_o, cor_o,
                    top_b, bot_b, fold_b, lft_b, rgt_b, hs, hn, hw, he, cor,
                    send_sem, recv_sem, local_sem):
    a = lax.axis_index("lat")
    b = lax.axis_index("lon")
    last = nlat - 1
    levels, rows, cols = t_ref.shape
    left = (b + nlon - 1) % nlon
    right = (b + 1) % nlon
    mirror = nlon - 1 - b
    ne = (2 * nlon - 2 - b) % nlon
    nw = (nlon - b) % nlon
    fold = a == last

    def dev(la, lo):
        return tuple(la if ax == "lat" else lo for ax in axes)

    def zero_south():
        hs[...] = jnp.zeros_like(hs)
        cor[0] = jnp.zeros_like(cor[0])
        cor[1] = jnp.zeros_like(cor[1])

    when(a == 0, zero_south)

    partners = [
        (a < last, (a + 1, b)), (a > 0, (a - 1, b)), (True, (a, left)), (True, (a, right)),
        (a < last, (a + 1, right)), (a < last, (a + 1, left)),
        (a > 0, (a - 1, right)), (a > 0, (a - 1, left)),
        (fold, (last, mirror)), (fold & (ne != b), (last, ne)), (fold & (nw != b), (last, nw)),
    ]
    barrier = pltpu.get_barrier_semaphore()
    for cond, target in partners:
        when(cond, lambda target=target: pl.semaphore_signal(
            barrier, 1, device_id=dev(*target), device_id_type=pl.DeviceIdType.MESH))

    ins = (t_ref, s_ref, u_ref, v_ref)

    def body(k, carry):
        wet = jnp.where(d_ref[...] > k, 1.0, 0.0).astype(jnp.float32)
        for n, ref in enumerate(ins):
            x = ref[k] * wet
            top_b[n, k] = x[0:2]
            bot_b[n, k] = x[rows - 2:rows]
            flipped = reverse_lanes(x[rows - 8:rows])
            fold_b[n, k, 0:1] = signs[n] * flipped[7:8]
            fold_b[n, k, 1:2] = signs[n] * flipped[6:7]
            xt = jnp.transpose(x)
            lft_b[n, k] = xt[0:2]
            rgt_b[n, k] = xt[cols - 2:cols]
        return carry

    lax.fori_loop(0, levels, body, 0)

    below = (a + last) // (last + 1)
    above = (2 * last - a) // (last + 1)
    at_fold = a // last
    ne_apart = ((2 * b + 2) % nlon + nlon - 1) // nlon
    nw_apart = ((2 * b) % nlon + nlon - 1) // nlon
    peers = 2 + 3 * below + 3 * above + at_fold * (1 + ne_apart + nw_apart)
    pl.semaphore_wait(barrier, peers)

    relations = [
        (a < last, a > 0, bot_b, hs, (a + 1, b)),
        (a > 0, a < last, top_b, hn, (a - 1, b)),
        (fold, fold, fold_b, hn, (last, mirror)),
        (True, True, lft_b, he, (a, left)),
        (True, True, rgt_b, hw, (a, right)),
        (a < last, a > 0, rgt_b.at[:, :, 1:2], cor.at[0], (a + 1, right)),
        (a < last, a > 0, lft_b.at[:, :, 0:1], cor.at[1], (a + 1, left)),
        (a > 0, a < last, rgt_b.at[:, :, 1:2], cor.at[2], (a - 1, right)),
        (a > 0, a < last, lft_b.at[:, :, 0:1], cor.at[3], (a - 1, left)),
        (fold & (ne != b), fold & (ne != b), rgt_b.at[:, :, 1:2], cor.at[3], (last, ne)),
        (fold & (nw != b), fold & (nw != b), lft_b.at[:, :, 0:1], cor.at[2], (last, nw)),
    ]
    copies = []
    for idx, (send, recv, src, dst, target) in enumerate(relations):
        copy = pltpu.make_async_remote_copy(
            src_ref=src, dst_ref=dst, send_sem=send_sem.at[idx], recv_sem=recv_sem.at[idx],
            device_id=dev(*target), device_id_type=pl.DeviceIdType.MESH)
        copies.append((send, recv, copy))
        when(send, copy.start)
    own = [
        (fold & (ne == b), pltpu.make_async_copy(rgt_b.at[:, :, 1:2], cor.at[3], local_sem.at[0])),
        (fold & (nw == b), pltpu.make_async_copy(lft_b.at[:, :, 0:1], cor.at[2], local_sem.at[1])),
    ]
    for cond, copy in own:
        when(cond, copy.start)
    for send, recv, copy in copies:
        when(send, copy.wait_send)
        when(recv, copy.wait_recv)
    for cond, copy in own:
        when(cond, copy.wait)
    hs_o[...] = hs[...]
    hn_o[...] = hn[...]
    hw_o[...] = hw[...]
    he_o[...] = he[...]
    cor_o[...] = cor[...]


def step_kernel(nlat, t_ref, s_ref, u_ref, v_ref, d_ref, f_ref, hs_ref, hn_ref, hw_ref, he_ref,
                cor_ref, to_ref, so_ref, uo_ref, vo_ref,
                base, vp1, vm1, vp2, vm2, accx, accy, mt):
    k = pl.program_id(0)
    frame, width = base.shape[1], base.shape[2]
    rows = t_ref.shape[1]
    at_lat = lax.axis_index("lat")
    south = at_lat > 0
    fold = at_lat == nlat - 1

    @pl.when(k == 0)
    def _():
        base[...] = jnp.zeros_like(base)
        accx[...] = jnp.zeros_like(accx)
        accy[...] = jnp.zeros_like(accy)
        mt[...] = jnp.zeros_like(mt)

    for n in range(4):
        mt[8 * n:8 * n + 2] = he_ref[n, 0]
        mt[8 * n + 2:8 * n + 4] = hw_ref[n, 0]
        for c in range(4):
            mt[8 * n + 4 + c:8 * n + 5 + c] = cor_ref[c, n, 0]
    tt = jnp.transpose(mt[...])
    sub = lax.broadcasted_iota(jnp.int32, (top, 1), 0)
    zeros = jnp.zeros((top, 1), jnp.float32)

    wet = jnp.where(d_ref[...] > k, 1.0, 0.0).astype(jnp.float32)
    lane = lax.broadcasted_iota(jnp.int32, (frame, width), 1)
    ins = (t_ref, s_ref, u_ref, v_ref)
    for n in range(4):
        base[n, top:top + rows, :] = ins[n][0] * wet
        base[n, top - 2:top, :] = jnp.where(south, hs_ref[n, 0], 0.0)
        base[n, top + rows:top + rows + 2, :] = hn_ref[n, 0]
        whole = base[n]

        def col(r):
            return tt[:, 8 * n + r:8 * n + r + 1]

        def last_of(r):
            return tt[rows - 1:rows, 8 * n + r:8 * n + r + 1]

        def first_of(r):
            return tt[0:1, 8 * n + r:8 * n + r + 1]

        low_sw = jnp.where((sub == top - 1) & south, last_of(4), 0.0)
        low_se = jnp.where((sub == top - 1) & south, last_of(5), 0.0)
        nw_val = jnp.where(fold, signs[n] * last_of(6), first_of(6))
        ne_val = jnp.where(fold, signs[n] * last_of(7), first_of(7))
        high_nw = jnp.where(sub == 0, nw_val, 0.0)
        high_ne = jnp.where(sub == 0, ne_val, 0.0)
        e0 = jnp.broadcast_to(jnp.concatenate([low_se, col(0), high_ne], 0), (frame, width))
        e1 = jnp.broadcast_to(jnp.concatenate([zeros, col(1), zeros], 0), (frame, width))
        w0 = jnp.broadcast_to(jnp.concatenate([zeros, col(2), zeros], 0), (frame, width))
        w1 = jnp.broadcast_to(jnp.concatenate([low_sw, col(3), high_nw], 0), (frame, width))
        vp1[n] = jnp.where(lane == width - 1, e0, pltpu.roll(whole, width - 1, 1))
        vm1[n] = jnp.where(lane == 0, w1, pltpu.roll(whole, 1, 1))
        vp2[n] = jnp.where(lane == width - 2, e0,
                           jnp.where(lane == width - 1, e1, pltpu.roll(whole, width - 2, 1)))
        vm2[n] = jnp.where(lane == 0, w0, jnp.where(lane == 1, w1, pltpu.roll(whole, 2, 1)))

    def at(ref, n, d):
        return ref[n, top + d:top + d + rows, :]

    centre = [at(base, n, 0) for n in range(4)]
    first, second = centre[2], centre[3]
    parts = []
    for n in range(4):
        east, west = at(vp1, n, 0), at(vm1, n, 0)
        north, south_ = at(base, n, 1), at(base, n, -1)
        carried = 0.5 * (first * (east - west) + second * (north - south_))
        smooth = (
            20.0 * centre[n]
            - 8.0 * (east + west + north + south_)
            + 2.0 * (at(vp1, n, 1) + at(vp1, n, -1) + at(vm1, n, 1) + at(vm1, n, -1))
            + at(base, n, 2) + at(base, n, -2) + at(vp2, n, 0) + at(vm2, n, 0)
        )
        parts.append((east, west, north, south_, carried, smooth))

    def density(a, b):
        return -0.2 * a + 0.8 * b

    dx = density(parts[0][0], parts[1][0]) - density(parts[0][1], parts[1][1])
    dy = density(parts[0][2], parts[1][2]) - density(parts[0][3], parts[1][3])
    totx = accx[...] + dx
    toty = accy[...] + dy
    accx[...] = totx
    accy[...] = toty
    grad_x = 0.5 * (totx - 0.5 * dx)
    grad_y = 0.5 * (toty - 0.5 * dy)
    coriolis = f_ref[...]
    to_ref[0] = (centre[0] - time_step * parts[0][4] - biharmonic * parts[0][5]) * wet
    so_ref[0] = (centre[1] - time_step * parts[1][4] - biharmonic * parts[1][5]) * wet
    uo_ref[0] = (
        first + time_step * (coriolis * second - grad_x - parts[2][4]) - biharmonic * parts[2][5]
    ) * wet
    vo_ref[0] = (
        second + time_step * (-coriolis * first - grad_y - parts[3][4]) - biharmonic * parts[3][5]
    ) * wet


def shards(axes, temp, salt, uvel, vvel, depth_levels):
    levels, rows_dev, cols_dev = temp.shape
    nlat = lax.axis_size("lat")
    nlon = lax.axis_size("lon")
    at_lat = lax.axis_index("lat")
    f32 = jnp.float32
    vmem = pl.BlockSpec(memory_space=pltpu.VMEM)
    strip = jax.ShapeDtypeStruct((4, levels, 2, cols_dev), f32)
    corners = jax.ShapeDtypeStruct((4, 4, levels, 1, cols_dev), f32)
    hs, hn, hw, he, cor = pl.pallas_call(
        functools.partial(exchange_kernel, axes, nlat, nlon),
        out_shape=[strip] * 4 + [corners],
        in_specs=[vmem] * 5,
        out_specs=[vmem] * 5,
        scratch_shapes=[pltpu.VMEM(strip.shape, f32)] * 9
        + [pltpu.VMEM(corners.shape, f32)]
        + [pltpu.SemaphoreType.DMA((11,)), pltpu.SemaphoreType.DMA((11,)),
           pltpu.SemaphoreType.DMA((2,))],
        compiler_params=pltpu.CompilerParams(
            collective_id=0, has_side_effects=True, vmem_limit_bytes=48 * 1024 * 1024),
    )(temp, salt, uvel, vvel, depth_levels)

    total_rows = rows_dev * nlat
    global_rows = (at_lat * rows_dev + jnp.arange(rows_dev, dtype=jnp.int32)).astype(f32)
    coriolis = (0.5 * jnp.sin(math.pi * (global_rows + 0.5) / total_rows - 0.5 * math.pi))[:, None]
    coriolis = jnp.broadcast_to(coriolis, (rows_dev, cols_dev))

    frame = rows_dev + 2 * top
    level_block = pl.BlockSpec((1, rows_dev, cols_dev), lambda k: (k, 0, 0))
    plane = pl.BlockSpec((rows_dev, cols_dev), lambda k: (0, 0))
    halo = pl.BlockSpec((4, 1, 2, cols_dev), lambda k: (0, k, 0, 0))
    corner = pl.BlockSpec((4, 4, 1, 1, cols_dev), lambda k: (0, 0, k, 0, 0))
    out = pl.pallas_call(
        functools.partial(step_kernel, nlat),
        grid=(levels,),
        in_specs=[level_block] * 4 + [plane] * 2 + [halo] * 4 + [corner],
        out_specs=[level_block] * 4,
        out_shape=[jax.ShapeDtypeStruct(temp.shape, f32)] * 4,
        scratch_shapes=[pltpu.VMEM((4, frame, cols_dev), f32)] * 5
        + [pltpu.VMEM((rows_dev, cols_dev), f32)] * 2
        + [pltpu.VMEM((cols_dev, cols_dev), f32)],
        compiler_params=pltpu.CompilerParams(dimension_semantics=("arbitrary",)),
    )(temp, salt, uvel, vvel, depth_levels, coriolis, hs, hn, hw, he, cor)
    return tuple(out)


def solution(mesh):
    placed = (
        P(None, "lat", "lon"),
        P(None, "lat", "lon"),
        P(None, "lat", "lon"),
        P(None, "lat", "lon"),
        P("lat", "lon"),
    )
    return jax.shard_map(
        functools.partial(shards, tuple(mesh.axis_names)),
        mesh=mesh,
        in_specs=placed,
        out_specs=(
            P(None, "lat", "lon"),
            P(None, "lat", "lon"),
            P(None, "lat", "lon"),
            P(None, "lat", "lon"),
        ),
        check_vma=False,
    )
```

time: 72.4 us -> 62.3 us (0.86)
  the two profiles are of different devices: /device:TPU:91 before, /device:TPU:32 now
where the time goes in v2:
time: 62.3 us; the launch traced here: 61.9 us
  Pallas kernels  52.4 us (84%)
  local copies, waits for them, and re-layouts  8.81 us (14%)
  between operations  0.67 us (1%)
    pallas_call x1, Pallas kernels, shards(): pl.pallas_call(functools.partial(exchange_kernel, axes, nlat, nlon), out_...  27.1 us
    pallas_call x1, Pallas kernels, shards(): pl.pallas_call(functools.partial(step_kernel, nlat), grid=(levels,), in_s...  25.3 us
    unnamed x20, local copies, waits for them, and re-layouts  8.09 us

profile of v2, /device:TPU:32, one launch (start us, length us, event | category | flops | bytes accessed | tf_op | source)
XLA Modules:
  0.0 61.9 jit_solution(10876082955316980040)
XLA Ops:
  0.6 0.0 copy-start.4
  0.7 0.7 %broadcast_in_dim.2.f_ref = f32[128,128]{1,0:T(8,128)} broadcast(f32[128]{0:T(128)S(1)} %sine_multiply_fusion), dimensions={0} | broadcast | bytes 66048 | tf_op jit(solution)/shard_map/broadcast_in_dim | solution.py:259
  1.4 0.1 copy-done.4
  1.5 0.0 copy-start
  1.5 1.2 %copy-done = f32[16,128,128]{2,1,0:T(8,128)S(1)} copy-done((f32[16,128,128]{2,1,0:T(8,128)S(1)}, f32[16,128,128]{2,1,0:T(8,128)}, u32[]{:S(2)}) %copy-start) | copy-done | bytes 1048600
  2.7 0.0 copy-start.1
  2.7 1.2 %copy-done.1 = f32[16,128,128]{2,1,0:T(8,128)S(1)} copy-done((f32[16,128,128]{2,1,0:T(8,128)S(1)}, f32[16,128,128]{2,1,0:T(8,128)}, u32[]{:S(2)}) %copy-start.1) | copy-done | bytes 1048600
  3.9 0.0 copy-start.2
  3.9 1.2 %copy-done.2 = f32[16,128,128]{2,1,0:T(8,128)S(1)} copy-done((f32[16,128,128]{2,1,0:T(8,128)S(1)}, f32[16,128,128]{2,1,0:T(8,128)}, u32[]{:S(2)}) %copy-start.2) | copy-done | bytes 1048600
  5.1 0.0 copy-start.3
  5.2 1.2 %copy-done.3 = f32[16,128,128]{2,1,0:T(8,128)S(1)} copy-done((f32[16,128,128]{2,1,0:T(8,128)S(1)}, f32[16,128,128]{2,1,0:T(8,128)}, u32[]{:S(2)}) %copy-start.3) | copy-done | bytes 1048600
  6.4 27.1 %shard_map.84 = (f32[4,16,2,128]{3,2,1,0:T(2,128)S(1)}, f32[4,16,2,128]{3,2,1,0:T(2,128)S(1)}, f32[4,16,2,128]{3,2,1,0:T(2,128)S(1)}, f32[4,16,2,128]{3,2,1,0:T(2,128)S(1)}, f32[4,4,16,1,128]{4,3,2,1,0:T(1,128)S(1)}) custom-call(f32[16,128,128]{2,1,0:T(8,128)S(1)} %copy-done, f32[16,128,128]{2,1,0:T(8,128)S(1)} %copy-done.1, f32[16,128,128]{2,1,0:T(8,128)S(1)} %copy-done.2, ...), custom_call_target="tpu_custom_call" | custom-call | tf_op jit(solution)/shard_map/pallas_call | solution.py:243
  33.5 0.0 copy-start.5
  33.5 0.6 %copy-done.5 = f32[4,4,16,1,128]{4,3,2,1,0:T(1,128)} copy-done((f32[4,4,16,1,128]{4,3,2,1,0:T(1,128)}, f32[4,4,16,1,128]{4,3,2,1,0:T(1,128)S(1)}, u32[]{:S(2)}) %copy-start.5) | copy-done | bytes 131096
  34.1 0.0 copy-start.6
  34.1 0.6 %copy-done.6 = f32[4,16,2,128]{3,2,1,0:T(2,128)} copy-done((f32[4,16,2,128]{3,2,1,0:T(2,128)}, f32[4,16,2,128]{3,2,1,0:T(2,128)S(1)}, u32[]{:S(2)}) %copy-start.6) | copy-done | bytes 65560
  34.8 0.0 copy-start.7
  34.8 0.6 %copy-done.7 = f32[4,16,2,128]{3,2,1,0:T(2,128)} copy-done((f32[4,16,2,128]{3,2,1,0:T(2,128)}, f32[4,16,2,128]{3,2,1,0:T(2,128)S(1)}, u32[]{:S(2)}) %copy-start.7) | copy-done | bytes 65560
  35.4 0.0 copy-start.8
  35.4 0.6 %copy-done.8 = f32[4,16,2,128]{3,2,1,0:T(2,128)} copy-done((f32[4,16,2,128]{3,2,1,0:T(2,128)}, f32[4,16,2,128]{3,2,1,0:T(2,128)S(1)}, u32[]{:S(2)}) %copy-start.8) | copy-done | bytes 65560
  36.0 0.0 copy-start.9
  36.0 0.6 %copy-done.9 = f32[4,16,2,128]{3,2,1,0:T(2,128)} copy-done((f32[4,16,2,128]{3,2,1,0:T(2,128)}, f32[4,16,2,128]{3,2,1,0:T(2,128)S(1)}, u32[]{:S(2)}) %copy-start.9) | copy-done | bytes 65560
  36.6 25.3 %shard_map.85 = (f32[16,128,128]{2,1,0:T(8,128)}, f32[16,128,128]{2,1,0:T(8,128)}, f32[16,128,128]{2,1,0:T(8,128)}, f32[16,128,128]{2,1,0:T(8,128)}) custom-call(f32[16,128,128]{2,1,0:T(8,128)} %t_ref.3, f32[16,128,128]{2,1,0:T(8,128)} %s_ref.3, f32[16,128,128]{2,1,0:T(8,128)} %u_ref.3, f32[16,128,128]{2,1,0:T(8,128)} %v_ref.3, s32[128,128]{1,0:T(8,128)} %d_ref.3, ...), custom_call_target="tpu_custom_call" | custom-call | tf_op jit(solution)/shard_map/pallas_call | solution.py:266
  (1 shorter events, 0.0 us)
Async XLA Ops:
  0.6 0.8 %copy-start.4 = (s32[128,128]{1,0:T(8,128)S(1)}, s32[128,128]{1,0:T(8,128)}, u32[]{:S(2)}) copy-start(s32[128,128]{1,0:T(8,128)} %d_ref.3) | copy-start | bytes 196612
  1.5 1.2 %copy-start = (f32[16,128,128]{2,1,0:T(8,128)S(1)}, f32[16,128,128]{2,1,0:T(8,128)}, u32[]{:S(2)}) copy-start(f32[16,128,128]{2,1,0:T(8,128)} %t_ref.3) | copy-start | bytes 3145732
  2.7 1.2 %copy-start.1 = (f32[16,128,128]{2,1,0:T(8,128)S(1)}, f32[16,128,128]{2,1,0:T(8,128)}, u32[]{:S(2)}) copy-start(f32[16,128,128]{2,1,0:T(8,128)} %s_ref.3) | copy-start | bytes 3145732
  3.9 1.2 %copy-start.2 = (f32[16,128,128]{2,1,0:T(8,128)S(1)}, f32[16,128,128]{2,1,0:T(8,128)}, u32[]{:S(2)}) copy-start(f32[16,128,128]{2,1,0:T(8,128)} %u_ref.3) | copy-start | bytes 3145732
  5.1 1.2 %copy-start.3 = (f32[16,128,128]{2,1,0:T(8,128)S(1)}, f32[16,128,128]{2,1,0:T(8,128)}, u32[]{:S(2)}) copy-start(f32[16,128,128]{2,1,0:T(8,128)} %v_ref.3) | copy-start | bytes 3145732
  33.5 0.6 %copy-start.5 = (f32[4,4,16,1,128]{4,3,2,1,0:T(1,128)}, f32[4,4,16,1,128]{4,3,2,1,0:T(1,128)S(1)}, u32[]{:S(2)}) copy-start(f32[4,4,16,1,128]{4,3,2,1,0:T(1,128)S(1)} %get-tuple-element.13.cor_ref) | copy-start | bytes 393220
  34.1 0.6 %copy-start.6 = (f32[4,16,2,128]{3,2,1,0:T(2,128)}, f32[4,16,2,128]{3,2,1,0:T(2,128)S(1)}, u32[]{:S(2)}) copy-start(f32[4,16,2,128]{3,2,1,0:T(2,128)S(1)} %get-tuple-element.9.hs_ref) | copy-start | bytes 196612
  34.8 0.6 %copy-start.7 = (f32[4,16,2,128]{3,2,1,0:T(2,128)}, f32[4,16,2,128]{3,2,1,0:T(2,128)S(1)}, u32[]{:S(2)}) copy-start(f32[4,16,2,128]{3,2,1,0:T(2,128)S(1)} %get-tuple-element.10.hn_ref) | copy-start | bytes 196612
  35.4 0.6 %copy-start.8 = (f32[4,16,2,128]{3,2,1,0:T(2,128)}, f32[4,16,2,128]{3,2,1,0:T(2,128)S(1)}, u32[]{:S(2)}) copy-start(f32[4,16,2,128]{3,2,1,0:T(2,128)S(1)} %get-tuple-element.11.hw_ref) | copy-start | bytes 196612
  36.0 0.6 %copy-start.9 = (f32[4,16,2,128]{3,2,1,0:T(2,128)}, f32[4,16,2,128]{3,2,1,0:T(2,128)S(1)}, u32[]{:S(2)}) copy-start(f32[4,16,2,128]{3,2,1,0:T(2,128)S(1)} %get-tuple-element.12.he_ref) | copy-start | bytes 196612

commit v3 on v2

--- a/solution.py
+++ b/solution.py
@@ -21,30 +21,21 @@
         pl.when(cond)(fn)
 
 
-def reverse_lanes(x):
-    lane = lax.broadcasted_iota(jnp.int32, x.shape, 1)
-    width = x.shape[1]
-    bit = 1
-    while bit < width:
-        x = jnp.where((lane & bit) != 0, pltpu.roll(x, bit, 1), pltpu.roll(x, width - bit, 1))
-        bit *= 2
-    return x
-
-
-def exchange_kernel(axes, nlat, nlon, t_ref, s_ref, u_ref, v_ref, d_ref,
+def exchange_kernel(axes, nlat, nlon, t_hbm, s_hbm, u_hbm, v_hbm, d_hbm,
                     hs_o, hn_o, hw_o, he_o, cor_o,
-                    top_b, bot_b, fold_b, lft_b, rgt_b, hs, hn, hw, he, cor,
-                    send_sem, recv_sem, local_sem):
+                    xin, d_ref, top_b, bot_b, lft_b, rgt_b, hs, hn, hw, he, cor,
+                    send_sem, recv_sem, in_sem):
     a = lax.axis_index("lat")
     b = lax.axis_index("lon")
     last = nlat - 1
-    levels, rows, cols = t_ref.shape
+    levels, rows, cols = t_hbm.shape
     left = (b + nlon - 1) % nlon
     right = (b + 1) % nlon
-    mirror = nlon - 1 - b
-    ne = (2 * nlon - 2 - b) % nlon
-    nw = (nlon - b) % nlon
-    fold = a == last
+    loads = [pltpu.make_async_copy(src, xin.at[n], in_sem.at[n])
+             for n, src in enumerate((t_hbm, s_hbm, u_hbm, v_hbm))]
+    loads.append(pltpu.make_async_copy(d_hbm, d_ref, in_sem.at[4]))
+    for copy in loads:
+        copy.start()
 
     def dev(la, lo):
         return tuple(la if ax == "lat" else lo for ax in axes)
@@ -56,28 +47,32 @@
 
     when(a == 0, zero_south)
 
+    def zero_north():
+        hn[...] = jnp.zeros_like(hn)
+        cor[2] = jnp.zeros_like(cor[2])
+        cor[3] = jnp.zeros_like(cor[3])
+
+    when(a == last, zero_north)
+
     partners = [
         (a < last, (a + 1, b)), (a > 0, (a - 1, b)), (True, (a, left)), (True, (a, right)),
         (a < last, (a + 1, right)), (a < last, (a + 1, left)),
         (a > 0, (a - 1, right)), (a > 0, (a - 1, left)),
-        (fold, (last, mirror)), (fold & (ne != b), (last, ne)), (fold & (nw != b), (last, nw)),
     ]
     barrier = pltpu.get_barrier_semaphore()
     for cond, target in partners:
         when(cond, lambda target=target: pl.semaphore_signal(
             barrier, 1, device_id=dev(*target), device_id_type=pl.DeviceIdType.MESH))
 
-    ins = (t_ref, s_ref, u_ref, v_ref)
+    for copy in loads:
+        copy.wait()
 
     def body(k, carry):
         wet = jnp.where(d_ref[...] > k, 1.0, 0.0).astype(jnp.float32)
-        for n, ref in enumerate(ins):
-            x = ref[k] * wet
+        for n in range(4):
+            x = xin[n, k] * wet
             top_b[n, k] = x[0:2]
             bot_b[n, k] = x[rows - 2:rows]
-            flipped = reverse_lanes(x[rows - 8:rows])
-            fold_b[n, k, 0:1] = signs[n] * flipped[7:8]
-            fold_b[n, k, 1:2] = signs[n] * flipped[6:7]
             xt = jnp.transpose(x)
             lft_b[n, k] = xt[0:2]
             rgt_b[n, k] = xt[cols - 2:cols]
@@ -87,24 +82,18 @@
 
     below = (a + last) // (last + 1)
     above = (2 * last - a) // (last + 1)
-    at_fold = a // last
-    ne_apart = ((2 * b + 2) % nlon + nlon - 1) // nlon
-    nw_apart = ((2 * b) % nlon + nlon - 1) // nlon
-    peers = 2 + 3 * below + 3 * above + at_fold * (1 + ne_apart + nw_apart)
+    peers = 2 + 3 * below + 3 * above
     pl.semaphore_wait(barrier, peers)
 
     relations = [
         (a < last, a > 0, bot_b, hs, (a + 1, b)),
         (a > 0, a < last, top_b, hn, (a - 1, b)),
-        (fold, fold, fold_b, hn, (last, mirror)),
         (True, True, lft_b, he, (a, left)),
         (True, True, rgt_b, hw, (a, right)),
         (a < last, a > 0, rgt_b.at[:, :, 1:2], cor.at[0], (a + 1, right)),
         (a < last, a > 0, lft_b.at[:, :, 0:1], cor.at[1], (a + 1, left)),
         (a > 0, a < last, rgt_b.at[:, :, 1:2], cor.at[2], (a - 1, right)),
         (a > 0, a < last, lft_b.at[:, :, 0:1], cor.at[3], (a - 1, left)),
-        (fold & (ne != b), fold & (ne != b), rgt_b.at[:, :, 1:2], cor.at[3], (last, ne)),
-        (fold & (nw != b), fold & (nw != b), lft_b.at[:, :, 0:1], cor.at[2], (last, nw)),
     ]
     copies = []
     for idx, (send, recv, src, dst, target) in enumerate(relations):
@@ -113,17 +102,9 @@
             device_id=dev(*target), device_id_type=pl.DeviceIdType.MESH)
         copies.append((send, recv, copy))
         when(send, copy.start)
-    own = [
-        (fold & (ne == b), pltpu.make_async_copy(rgt_b.at[:, :, 1:2], cor.at[3], local_sem.at[0])),
-        (fold & (nw == b), pltpu.make_async_copy(lft_b.at[:, :, 0:1], cor.at[2], local_sem.at[1])),
-    ]
-    for cond, copy in own:
-        when(cond, copy.start)
     for send, recv, copy in copies:
         when(send, copy.wait_send)
         when(recv, copy.wait_recv)
-    for cond, copy in own:
-        when(cond, copy.wait)
     hs_o[...] = hs[...]
     hn_o[...] = hn[...]
     hw_o[...] = hw[...]
@@ -132,7 +113,7 @@
 
 
 def step_kernel(nlat, t_ref, s_ref, u_ref, v_ref, d_ref, f_ref, hs_ref, hn_ref, hw_ref, he_ref,
-                cor_ref, to_ref, so_ref, uo_ref, vo_ref,
+                cor_ref, fr_ref, fc_ref, to_ref, so_ref, uo_ref, vo_ref,
                 base, vp1, vm1, vp2, vm2, accx, accy, mt):
     k = pl.program_id(0)
     frame, width = base.shape[1], base.shape[2]
@@ -163,7 +144,7 @@
     for n in range(4):
         base[n, top:top + rows, :] = ins[n][0] * wet
         base[n, top - 2:top, :] = jnp.where(south, hs_ref[n, 0], 0.0)
-        base[n, top + rows:top + rows + 2, :] = hn_ref[n, 0]
+        base[n, top + rows:top + rows + 2, :] = jnp.where(fold, fr_ref[n, 0], hn_ref[n, 0])
         whole = base[n]
 
         def col(r):
@@ -177,8 +158,8 @@
 
         low_sw = jnp.where((sub == top - 1) & south, last_of(4), 0.0)
         low_se = jnp.where((sub == top - 1) & south, last_of(5), 0.0)
-        nw_val = jnp.where(fold, signs[n] * last_of(6), first_of(6))
-        ne_val = jnp.where(fold, signs[n] * last_of(7), first_of(7))
+        nw_val = jnp.where(fold, fc_ref[n, 0, 0:1, 0:1], first_of(6))
+        ne_val = jnp.where(fold, fc_ref[n, 0, 0:1, 1:2], first_of(7))
         high_nw = jnp.where(sub == 0, nw_val, 0.0)
         high_ne = jnp.where(sub == 0, ne_val, 0.0)
         e0 = jnp.broadcast_to(jnp.concatenate([low_se, col(0), high_ne], 0), (frame, width))
@@ -240,15 +221,34 @@
     vmem = pl.BlockSpec(memory_space=pltpu.VMEM)
     strip = jax.ShapeDtypeStruct((4, levels, 2, cols_dev), f32)
     corners = jax.ShapeDtypeStruct((4, 4, levels, 1, cols_dev), f32)
+    fields = (temp, salt, uvel, vvel)
+    level_index = jnp.arange(levels, dtype=jnp.int32)[:, None, None]
+    wet_tail = jnp.where(depth_levels[None, rows_dev - 2:, :] > level_index, 1.0, 0.0).astype(f32)
+    tail = jnp.stack([x[:, rows_dev - 2:, :] * wet_tail for x in fields])
+    sign = jnp.array(signs, f32)[:, None, None, None]
+    piece = tail[:, :, ::-1, ::-1] * sign
+    ends = jnp.concatenate([tail[:, :, 1:, :1], tail[:, :, 1:, -1:]], axis=3) * sign
+    last = nlat - 1
+
+    def on_fold(value, target):
+        pairs = [(i * nlat + last, target(i) * nlat + last) for i in range(nlon)]
+        return lax.ppermute(value, ("lon", "lat"), pairs)
+
+    fold_rows = on_fold(piece, lambda i: nlon - 1 - i)
+    fold_nw = on_fold(ends[..., 0:1], lambda i: (nlon - i) % nlon)
+    fold_ne = on_fold(ends[..., 1:2], lambda i: (2 * nlon - 2 - i) % nlon)
+    fold_corners = jnp.concatenate([fold_nw, fold_ne], axis=3)
     hs, hn, hw, he, cor = pl.pallas_call(
         functools.partial(exchange_kernel, axes, nlat, nlon),
         out_shape=[strip] * 4 + [corners],
-        in_specs=[vmem] * 5,
+        in_specs=[pl.BlockSpec(memory_space=pl.ANY)] * 5,
         out_specs=[vmem] * 5,
-        scratch_shapes=[pltpu.VMEM(strip.shape, f32)] * 9
+        scratch_shapes=[pltpu.VMEM((4,) + temp.shape, f32),
+                        pltpu.VMEM(depth_levels.shape, jnp.int32)]
+        + [pltpu.VMEM(strip.shape, f32)] * 8
         + [pltpu.VMEM(corners.shape, f32)]
-        + [pltpu.SemaphoreType.DMA((11,)), pltpu.SemaphoreType.DMA((11,)),
-           pltpu.SemaphoreType.DMA((2,))],
+        + [pltpu.SemaphoreType.DMA((8,)), pltpu.SemaphoreType.DMA((8,)),
+           pltpu.SemaphoreType.DMA((5,))],
         compiler_params=pltpu.CompilerParams(
             collective_id=0, has_side_effects=True, vmem_limit_bytes=48 * 1024 * 1024),
     )(temp, salt, uvel, vvel, depth_levels)
@@ -263,17 +263,18 @@
     plane = pl.BlockSpec((rows_dev, cols_dev), lambda k: (0, 0))
     halo = pl.BlockSpec((4, 1, 2, cols_dev), lambda k: (0, k, 0, 0))
     corner = pl.BlockSpec((4, 4, 1, 1, cols_dev), lambda k: (0, 0, k, 0, 0))
+    fold_corner = pl.BlockSpec((4, 1, 1, 2), lambda k: (0, k, 0, 0))
     out = pl.pallas_call(
         functools.partial(step_kernel, nlat),
         grid=(levels,),
-        in_specs=[level_block] * 4 + [plane] * 2 + [halo] * 4 + [corner],
+        in_specs=[level_block] * 4 + [plane] * 2 + [halo] * 4 + [corner, halo, fold_corner],
         out_specs=[level_block] * 4,
         out_shape=[jax.ShapeDtypeStruct(temp.shape, f32)] * 4,
         scratch_shapes=[pltpu.VMEM((4, frame, cols_dev), f32)] * 5
         + [pltpu.VMEM((rows_dev, cols_dev), f32)] * 2
         + [pltpu.VMEM((cols_dev, cols_dev), f32)],
         compiler_params=pltpu.CompilerParams(dimension_semantics=("arbitrary",)),
-    )(temp, salt, uvel, vvel, depth_levels, coriolis, hs, hn, hw, he, cor)
+    )(temp, salt, uvel, vvel, depth_levels, coriolis, hs, hn, hw, he, cor, fold_rows, fold_corners)
     return tuple(out)
 
 

time: 62.3 us -> 74.3 us (1.19)
  the two profiles are of different devices: /device:TPU:32 before, /device:TPU:100 now
where the time goes in v3:
time: 74.3 us; the launch traced here: 73.8 us
  Pallas kernels  58.5 us (79%)
  local copies, waits for them, and re-layouts  11.4 us (15%)
  starting transfers between devices  1.98 us (3%)
  other arithmetic  1.22 us (2%)
    pallas_call x1, Pallas kernels, shards(): pl.pallas_call(functools.partial(step_kernel, nlat), grid=(levels,), in_s...  29.7 us
    pallas_call x1, Pallas kernels, shards(): pl.pallas_call(functools.partial(exchange_kernel, axes, nlat, nlon), out_...  28.8 us
    unnamed x24, local copies, waits for them, and re-layouts  8.64 us
    ppermute x3, starting transfers between devices, on_fold(): return lax.ppermute(value, ('lon', 'lat'), pairs)  1.98 us
  transfers between devices with their start and end apart: 3, of which 0 were waited for; matrix products, arithmetic and copies ran while one was open for 2% of the time, Pallas kernels for 39%

profile of v3, /device:TPU:100, one launch (start us, length us, event | category | flops | bytes accessed | tf_op | source)
XLA Modules:
  0.0 73.8 jit_solution(3665302095933814107)
XLA Ops:
  0.6 0.7 slice.28
  1.3 1.0 %multiply_bitcast_fusion.3 = (f32[1,16,2,128]{3,2,1,0:T(2,128)S(1)}, f32[1,16,2,128]{3,2,1,0:T(2,128)S(1)}, f32[1,16,2,128]{3,2,1,0:T(2,128)S(1)}, f32[1,16,2,128]{3,2,1,0:T(2,128)S(1)}) fusion(f32[16,128,128]{2,1,0:T(8,128)} %t_ref.1, s32[2,128]{1,0:T(2,128)S(1)} %slice.28, f32[16,128,128]{2,1,0:T(8,128)} %v_ref.1, f32[16,128,128]{2,1,0:T(8,128)} %u_ref.1, ...), kind=kLoop, calls=%fused_computation.6 | loop fusion | flops 24576 | bytes 132096 | tf_op jit(solution)/shard_map/stack | solution.py:227
  2.3 0.1 fusion
  2.5 0.1 copy.10
  2.6 0.0 copy-start.11
  2.6 0.1 copy.11
  2.7 0.6 copy-done.11
  3.2 0.1 maximum_multiply_fusion
  3.3 0.6 collective-permute-start.1
  4.0 0.7 collective-permute-start.2
  4.6 0.3 rev.3
  4.9 0.0 copy-start.4
  4.9 0.1 broadcast_multiply_fusion
  5.0 0.7 collective-permute-start
  5.8 0.0 copy-done.4
  5.8 0.0 copy-start
  5.8 1.2 %copy-done = f32[16,128,128]{2,1,0:T(8,128)S(1)} copy-done((f32[16,128,128]{2,1,0:T(8,128)S(1)}, f32[16,128,128]{2,1,0:T(8,128)}, u32[]{:S(2)}) %copy-start) | copy-done | bytes 1048600
  7.0 0.0 copy-start.1
  7.0 1.2 %copy-done.1 = f32[16,128,128]{2,1,0:T(8,128)S(1)} copy-done((f32[16,128,128]{2,1,0:T(8,128)S(1)}, f32[16,128,128]{2,1,0:T(8,128)}, u32[]{:S(2)}) %copy-start.1) | copy-done | bytes 1048600
  8.2 0.0 copy-start.2
  8.2 1.2 %copy-done.2 = f32[16,128,128]{2,1,0:T(8,128)S(1)} copy-done((f32[16,128,128]{2,1,0:T(8,128)S(1)}, f32[16,128,128]{2,1,0:T(8,128)}, u32[]{:S(2)}) %copy-start.2) | copy-done | bytes 1048600
  9.5 0.0 copy-start.3
  9.5 1.2 %copy-done.3 = f32[16,128,128]{2,1,0:T(8,128)S(1)} copy-done((f32[16,128,128]{2,1,0:T(8,128)S(1)}, f32[16,128,128]{2,1,0:T(8,128)}, u32[]{:S(2)}) %copy-start.3) | copy-done | bytes 1048600
  10.7 28.8 %shard_map.93 = (f32[4,16,2,128]{3,2,1,0:T(2,128)S(1)}, f32[4,16,2,128]{3,2,1,0:T(2,128)S(1)}, f32[4,16,2,128]{3,2,1,0:T(2,128)S(1)}, f32[4,16,2,128]{3,2,1,0:T(2,128)S(1)}, f32[4,4,16,1,128]{4,3,2,1,0:T(1,128)S(1)}) custom-call(f32[16,128,128]{2,1,0:T(8,128)S(1)} %copy-done, f32[16,128,128]{2,1,0:T(8,128)S(1)} %copy-done.1, f32[16,128,128]{2,1,0:T(8,128)S(1)} %copy-done.2, ...), custom_call_target="tpu_custom_call" | custom-call | tf_op jit(solution)/shard_map/pallas_call | solution.py:241
  39.5 0.0 copy-start.5
  39.5 0.7 copy-done.5
  40.2 0.0 copy-start.6
  40.2 0.6 copy-done.6
  40.8 0.0 copy-start.7
  40.8 0.6 copy-done.7
  41.4 0.0 copy-start.8
  41.4 0.6 copy-done.8
  42.0 0.0 copy-start.9
  42.0 0.6 copy-done.9
  42.7 0.0 collective-permute-done.1
  42.7 0.0 collective-permute-done.2
  42.7 0.7 copy.12.fc_ref
  43.4 0.0 collective-permute-done.fr_ref
  43.4 0.0 copy-start.10
  43.4 0.7 broadcast_in_dim.10.f_ref
  44.1 0.0 copy-done.10
  44.1 29.7 %shard_map.94 = (f32[16,128,128]{2,1,0:T(8,128)}, f32[16,128,128]{2,1,0:T(8,128)}, f32[16,128,128]{2,1,0:T(8,128)}, f32[16,128,128]{2,1,0:T(8,128)}) custom-call(f32[16,128,128]{2,1,0:T(8,128)} %t_ref.1, f32[16,128,128]{2,1,0:T(8,128)} %s_ref.1, f32[16,128,128]{2,1,0:T(8,128)} %u_ref.1, f32[16,128,128]{2,1,0:T(8,128)} %v_ref.1, s32[128,128]{1,0:T(8,128)} %d_ref.1, ...), custom_call_target="tpu_custom_call" | custom-call | tf_op jit(solution)/shard_map/pallas_call | solution.py:267
  (4 shorter events, 0.1 us)
Async XLA Ops:
  2.6 0.7 copy-start.11
  3.3 39.3 %collective-permute-start.1 = (f32[4,16,1,1]{1,0,3,2:T(4,128)S(1)}, f32[4,16,1,1]{1,0,3,2:T(4,128)S(1)}, u32[]{:S(2)}, u32[]{:S(2)}) collective-permute-start(f32[4,16,1,1]{1,0,3,2:T(4,128)S(1)} %get-tuple-element.16), channel_id=1, source_target_pairs={{7,7},{15,255},{23,247},{31,239},{39,231},{47,223},{55,215},{63,20... | collective-permute-start | bytes 776 | tf_op jit(solution)/shard_map/ppermute | solution.py:235
  4.0 38.7 %collective-permute-start.2 = (f32[4,16,1,1]{1,0,3,2:T(4,128)S(1)}, f32[4,16,1,1]{1,0,3,2:T(4,128)S(1)}, u32[]{:S(2)}, u32[]{:S(2)}) collective-permute-start(f32[4,16,1,1]{1,0,3,2:T(4,128)S(1)} %get-tuple-element.17), channel_id=1, source_target_pairs={{7,247},{15,239},{23,231},{31,223},{39,215},{47,207},{55,199},{63,... | collective-permute-start | bytes 776 | tf_op jit(solution)/shard_map/ppermute | solution.py:235
  4.9 0.8 %copy-start.4 = (s32[128,128]{1,0:T(8,128)S(1)}, s32[128,128]{1,0:T(8,128)}, u32[]{:S(2)}) copy-start(s32[128,128]{1,0:T(8,128)} %d_ref.1) | copy-start | bytes 196612
  5.0 38.3 %collective-permute-start = (f32[4,16,2,128]{3,2,1,0:T(2,128)S(1)}, f32[4,16,2,128]{3,2,1,0:T(2,128)S(1)}, u32[]{:S(2)}, u32[]{:S(2)}) collective-permute-start(f32[4,16,2,128]{3,2,1,0:T(2,128)S(1)} %broadcast_multiply_fusion), channel_id=1, source_target_pairs={{7,255},{15,247},{23,239},{31,231},{39,223},{47,215},{55,207},{63,... | collective-permute-start | bytes 196616 | tf_op jit(solution)/shard_map/ppermute | solution.py:235
  5.8 1.2 %copy-start = (f32[16,128,128]{2,1,0:T(8,128)S(1)}, f32[16,128,128]{2,1,0:T(8,128)}, u32[]{:S(2)}) copy-start(f32[16,128,128]{2,1,0:T(8,128)} %t_ref.1) | copy-start | bytes 3145732
  7.0 1.2 %copy-start.1 = (f32[16,128,128]{2,1,0:T(8,128)S(1)}, f32[16,128,128]{2,1,0:T(8,128)}, u32[]{:S(2)}) copy-start(f32[16,128,128]{2,1,0:T(8,128)} %s_ref.1) | copy-start | bytes 3145732
  8.2 1.2 %copy-start.2 = (f32[16,128,128]{2,1,0:T(8,128)S(1)}, f32[16,128,128]{2,1,0:T(8,128)}, u32[]{:S(2)}) copy-start(f32[16,128,128]{2,1,0:T(8,128)} %u_ref.1) | copy-start | bytes 3145732
  9.5 1.2 %copy-start.3 = (f32[16,128,128]{2,1,0:T(8,128)S(1)}, f32[16,128,128]{2,1,0:T(8,128)}, u32[]{:S(2)}) copy-start(f32[16,128,128]{2,1,0:T(8,128)} %v_ref.1) | copy-start | bytes 3145732
  39.5 0.7 copy-start.5
  40.2 0.6 copy-start.6
  40.8 0.6 copy-start.7
  41.4 0.6 copy-start.8
  42.0 0.6 copy-start.9
  43.4 0.7 copy-start.10

commit v4 on v3

--- a/solution.py
+++ b/solution.py
@@ -130,10 +130,10 @@
         mt[...] = jnp.zeros_like(mt)
 
     for n in range(4):
-        mt[8 * n:8 * n + 2] = he_ref[n, 0]
-        mt[8 * n + 2:8 * n + 4] = hw_ref[n, 0]
+        mt[8 * n:8 * n + 2] = he_ref[n, k]
+        mt[8 * n + 2:8 * n + 4] = hw_ref[n, k]
         for c in range(4):
-            mt[8 * n + 4 + c:8 * n + 5 + c] = cor_ref[c, n, 0]
+            mt[8 * n + 4 + c:8 * n + 5 + c] = cor_ref[c, n, k]
     tt = jnp.transpose(mt[...])
     sub = lax.broadcasted_iota(jnp.int32, (top, 1), 0)
     zeros = jnp.zeros((top, 1), jnp.float32)
@@ -143,8 +143,8 @@
     ins = (t_ref, s_ref, u_ref, v_ref)
     for n in range(4):
         base[n, top:top + rows, :] = ins[n][0] * wet
-        base[n, top - 2:top, :] = jnp.where(south, hs_ref[n, 0], 0.0)
-        base[n, top + rows:top + rows + 2, :] = jnp.where(fold, fr_ref[n, 0], hn_ref[n, 0])
+        base[n, top - 2:top, :] = jnp.where(south, hs_ref[n, k], 0.0)
+        base[n, top + rows:top + rows + 2, :] = jnp.where(fold, fr_ref[n, k], hn_ref[n, k])
         whole = base[n]
 
         def col(r):
@@ -158,8 +158,9 @@
 
         low_sw = jnp.where((sub == top - 1) & south, last_of(4), 0.0)
         low_se = jnp.where((sub == top - 1) & south, last_of(5), 0.0)
-        nw_val = jnp.where(fold, fc_ref[n, 0, 0:1, 0:1], first_of(6))
-        ne_val = jnp.where(fold, fc_ref[n, 0, 0:1, 1:2], first_of(7))
+        fold_pair = fc_ref[n, k]
+        nw_val = jnp.where(fold, fold_pair[:, 0:1], first_of(6))
+        ne_val = jnp.where(fold, fold_pair[:, 1:2], first_of(7))
         high_nw = jnp.where(sub == 0, nw_val, 0.0)
         high_ne = jnp.where(sub == 0, ne_val, 0.0)
         e0 = jnp.broadcast_to(jnp.concatenate([low_se, col(0), high_ne], 0), (frame, width))
@@ -249,8 +250,7 @@
         + [pltpu.VMEM(corners.shape, f32)]
         + [pltpu.SemaphoreType.DMA((8,)), pltpu.SemaphoreType.DMA((8,)),
            pltpu.SemaphoreType.DMA((5,))],
-        compiler_params=pltpu.CompilerParams(
-            collective_id=0, has_side_effects=True, vmem_limit_bytes=48 * 1024 * 1024),
+        compiler_params=pltpu.CompilerParams(collective_id=0, has_side_effects=True),
     )(temp, salt, uvel, vvel, depth_levels)
 
     total_rows = rows_dev * nlat
@@ -261,13 +261,10 @@
     frame = rows_dev + 2 * top
     level_block = pl.BlockSpec((1, rows_dev, cols_dev), lambda k: (k, 0, 0))
     plane = pl.BlockSpec((rows_dev, cols_dev), lambda k: (0, 0))
-    halo = pl.BlockSpec((4, 1, 2, cols_dev), lambda k: (0, k, 0, 0))
-    corner = pl.BlockSpec((4, 4, 1, 1, cols_dev), lambda k: (0, 0, k, 0, 0))
-    fold_corner = pl.BlockSpec((4, 1, 1, 2), lambda k: (0, k, 0, 0))
     out = pl.pallas_call(
         functools.partial(step_kernel, nlat),
         grid=(levels,),
-        in_specs=[level_block] * 4 + [plane] * 2 + [halo] * 4 + [corner, halo, fold_corner],
+        in_specs=[level_block] * 4 + [plane] * 2 + [vmem] * 7,
         out_specs=[level_block] * 4,
         out_shape=[jax.ShapeDtypeStruct(temp.shape, f32)] * 4,
         scratch_shapes=[pltpu.VMEM((4, frame, cols_dev), f32)] * 5

time: 74.3 us -> 66.5 us (0.90)
  the two profiles are of different devices: /device:TPU:100 before, /device:TPU:31 now
where the time goes in v4:
time: 66.5 us; the launch traced here: 66.2 us
  Pallas kernels  59 us (89%)
  local copies, waits for them, and re-layouts  3.3 us (5%)
  starting transfers between devices  1.98 us (3%)
  other arithmetic  1.22 us (2%)
  between operations  0.71 us (1%)
    pallas_call x1, Pallas kernels, shards(): pl.pallas_call(functools.partial(step_kernel, nlat), grid=(levels,), in_s...  29.6 us
    pallas_call x1, Pallas kernels, shards(): pl.pallas_call(functools.partial(exchange_kernel, axes, nlat, nlon), out_...  29.4 us
    ppermute x3, starting transfers between devices, on_fold(): return lax.ppermute(value, ('lon', 'lat'), pairs)  1.98 us
  transfers between devices with their start and end apart: 3, of which 0 were waited for; matrix products, arithmetic and copies ran while one was open for 2% of the time, Pallas kernels for 44%

profile of v4, /device:TPU:31, one launch (start us, length us, event | category | flops | bytes accessed | tf_op | source)
XLA Modules:
  0.0 66.2 jit_solution(6664912738938016476)
XLA Ops:
  0.6 0.7 %slice.28 = s32[2,128]{1,0:T(2,128)S(1)} slice(s32[128,128]{1,0:T(8,128)} %d_ref.1), slice={[126:128], [0:128]} | slice | bytes 2048 | tf_op jit(solution)/shard_map/slice | solution.py:227
  1.3 1.0 %multiply_bitcast_fusion.3 = (f32[1,16,2,128]{3,2,1,0:T(2,128)S(1)}, f32[1,16,2,128]{3,2,1,0:T(2,128)S(1)}, f32[1,16,2,128]{3,2,1,0:T(2,128)S(1)}, f32[1,16,2,128]{3,2,1,0:T(2,128)S(1)}) fusion(f32[16,128,128]{2,1,0:T(8,128)} %t_ref.1, s32[2,128]{1,0:T(2,128)S(1)} %slice.28, f32[16,128,128]{2,1,0:T(8,128)} %v_ref.1, f32[16,128,128]{2,1,0:T(8,128)} %u_ref.1, ...), kind=kLoop, calls=%fused_computation.6 | loop fusion | flops 24576 | bytes 132096 | tf_op jit(solution)/shard_map/stack | solution.py:228
  2.3 0.1 fusion
  2.5 0.1 copy.10
  2.6 0.0 copy-start.1
  2.6 0.1 copy.11
  2.7 0.6 copy-done.1
  3.2 0.1 maximum_multiply_fusion
  3.3 0.6 collective-permute-start.1
  4.0 0.7 collective-permute-start.2
  4.6 0.3 rev.3
  4.9 0.1 broadcast_multiply_fusion
  5.0 0.7 %collective-permute-start = (f32[4,16,2,128]{3,2,1,0:T(2,128)S(1)}, f32[4,16,2,128]{3,2,1,0:T(2,128)S(1)}, u32[]{:S(2)}, u32[]{:S(2)}) collective-permute-start(f32[4,16,2,128]{3,2,1,0:T(2,128)S(1)} %broadcast_multiply_fusion), channel_id=1, source_target_pairs={{7,255},{15,247},{23,239},{31,231},{39,223},{47,215},{55,207},{63,... | collective-permute-start | bytes 196616 | tf_op jit(solution)/shard_map/ppermute | solution.py:236
  5.8 29.4 %shard_map.93 = (f32[4,16,2,128]{3,2,1,0:T(2,128)}, f32[4,16,2,128]{3,2,1,0:T(2,128)}, f32[4,16,2,128]{3,2,1,0:T(2,128)}, f32[4,16,2,128]{3,2,1,0:T(2,128)}, f32[4,4,16,1,128]{4,3,2,1,0:T(1,128)}) custom-call(f32[16,128,128]{2,1,0:T(8,128)} %t_ref.1, f32[16,128,128]{2,1,0:T(8,128)} %s_ref.1, f32[16,128,128]{2,1,0:T(8,128)} %u_ref.1, f32[16,128,128]{2,1,0:T(8,128)} %v_ref.1, ...), custom_call_target="tpu_custom_call" | custom-call | tf_op jit(solution)/shard_map/pallas_call | solution.py:242
  35.2 0.0 collective-permute-done.1
  35.2 0.0 collective-permute-done.2
  35.2 0.7 %copy.12.fc_ref = f32[4,16,1,2]{3,2,1,0:T(1,128)} copy(f32[4,16,1,2]{1,0,3,2:T(4,128)S(1)} %pad_maximum_fusion.1) | data formatting | bytes 1024 | tf_op jit(solution)/shard_map/concatenate | solution.py:241
  35.9 0.0 collective-permute-done.fr_ref
  35.9 0.0 copy-start
  36.0 0.7 %broadcast_in_dim.10.f_ref = f32[128,128]{1,0:T(8,128)} broadcast(f32[128]{0:T(128)S(1)} %sine_multiply_fusion), dimensions={0} | broadcast | bytes 66048 | tf_op jit(solution)/shard_map/broadcast_in_dim | solution.py:259
  36.7 0.0 copy-done
  36.7 29.6 %shard_map.94 = (f32[16,128,128]{2,1,0:T(8,128)}, f32[16,128,128]{2,1,0:T(8,128)}, f32[16,128,128]{2,1,0:T(8,128)}, f32[16,128,128]{2,1,0:T(8,128)}) custom-call(f32[16,128,128]{2,1,0:T(8,128)} %t_ref.1, f32[16,128,128]{2,1,0:T(8,128)} %s_ref.1, f32[16,128,128]{2,1,0:T(8,128)} %u_ref.1, f32[16,128,128]{2,1,0:T(8,128)} %v_ref.1, s32[128,128]{1,0:T(8,128)} %d_ref.1, ...), custom_call_target="tpu_custom_call" | custom-call | tf_op jit(solution)/shard_map/pallas_call | solution.py:264
  (4 shorter events, 0.1 us)
Async XLA Ops:
  2.6 0.7 copy-start.1
  3.3 31.9 %collective-permute-start.1 = (f32[4,16,1,1]{1,0,3,2:T(4,128)S(1)}, f32[4,16,1,1]{1,0,3,2:T(4,128)S(1)}, u32[]{:S(2)}, u32[]{:S(2)}) collective-permute-start(f32[4,16,1,1]{1,0,3,2:T(4,128)S(1)} %get-tuple-element.16), channel_id=1, source_target_pairs={{7,7},{15,255},{23,247},{31,239},{39,231},{47,223},{55,215},{63,20... | collective-permute-start | bytes 776 | tf_op jit(solution)/shard_map/ppermute | solution.py:236
  4.0 31.3 %collective-permute-start.2 = (f32[4,16,1,1]{1,0,3,2:T(4,128)S(1)}, f32[4,16,1,1]{1,0,3,2:T(4,128)S(1)}, u32[]{:S(2)}, u32[]{:S(2)}) collective-permute-start(f32[4,16,1,1]{1,0,3,2:T(4,128)S(1)} %get-tuple-element.17), channel_id=1, source_target_pairs={{7,247},{15,239},{23,231},{31,223},{39,215},{47,207},{55,199},{63,... | collective-permute-start | bytes 776 | tf_op jit(solution)/shard_map/ppermute | solution.py:236
  5.0 30.9 %collective-permute-start = (f32[4,16,2,128]{3,2,1,0:T(2,128)S(1)}, f32[4,16,2,128]{3,2,1,0:T(2,128)S(1)}, u32[]{:S(2)}, u32[]{:S(2)}) collective-permute-start(f32[4,16,2,128]{3,2,1,0:T(2,128)S(1)} %broadcast_multiply_fusion), channel_id=1, source_target_pairs={{7,255},{15,247},{23,239},{31,231},{39,223},{47,215},{55,207},{63,... | collective-permute-start | bytes 196616 | tf_op jit(solution)/shard_map/ppermute | solution.py:236
  35.9 0.7 %copy-start = (f32[4,16,2,128]{3,2,1,0:T(2,128)}, f32[4,16,2,128]{3,2,1,0:T(2,128)S(1)}, u32[]{:S(2)}) copy-start(f32[4,16,2,128]{3,2,1,0:T(2,128)S(1)} %collective-permute-done.fr_ref) | copy-start | bytes 196612
